TPU v7x, 128 devices: a whole 4x4x4 slice. The times are simulated.
128 devices in a mesh: blk: 32 (over x, y, core), mp: 4 (over z).
Axes of the slice: x: 4, y: 4, z: 4, core: 2. Of those that a mesh axis runs over, the one named last changes fastest.
Arguments:
- hidden: bfloat16 [144, 3584], replicated, may hold values from -6 to 6
- medusa_w: bfloat16 [2, 3584, 3584], P(None, 'blk', 'mp'), may hold values from -0.09375 to 0.09375
- embedding: bfloat16 [131072, 3584], P(('blk', 'mp')), may hold values from -0.5 to 0.5
- cand_ids: int32 [2, 144, 10], replicated, may hold values from 0 to 131071
- tree_q: bfloat16 [12, 48, 4096], P(None, None, 'mp'), may hold values from -6 to 6
- tree_key_value: bfloat16 [2, 12, 48, 2048], P(None, None, None, 'mp'), may hold values from -6 to 6
- prompt_key_value: bfloat16 [2, 32, 2048, 2048], P(None, 'blk', None, 'mp'), may hold values from -6 to 6
- block_group: int32 [32], P('blk'), may hold values from 0 to 11, as said below
- block_len: int32 [32], P('blk'), may hold values from 1 to 2048
- block_empty: int32 [32], P('blk'), may hold values 0 or 1
- parents: int32 [12, 48], replicated, may hold values from 0 to 46, as said below
- out_weight: bfloat16 [4096, 3584], P('mp'), may hold values from -0.09375 to 0.09375
- post_gain: float32 [3584], replicated, may hold values from 0.5 to 1.5
- resid: bfloat16 [576, 3584], P('blk'), may hold values from -6 to 6
Outputs:
- draft_logprob: float32 [2, 144, 10], replicated
- layer_out: bfloat16 [576, 3584], P('blk')
Inputs may be any that keep to these rules, and one draw needn't show every extreme that they name: `block_group`: every group number from 0 to min(12, 32) - 1 owns at least one block. `parents`: entry 0 of each row is 0; entry i for i >= 1 is below i; some group's last token has parent 48 - 2.
All inputs are finite; a program needn't handle non-finite values. No bound on the sum of `block_empty` on one device may be relied on, other than what follows from the above.
Results may differ from a plain program's by a relative error of at most 0.005.
Values may be sent and summed in bfloat16 or wider, within the bound.
A program may use at most 128 MiB of HBM per device.

v0:
```python
import jax
import jax.numpy as jnp
from jax import lax
from jax.sharding import PartitionSpec as P

HEAD_SIZE = 256


def capped(values, limit):
    return limit * jnp.tanh(values / limit)


def ancestry(parents):
    count = parents.shape[1]
    column = jnp.arange(count, dtype=jnp.int32)
    linked = (parents[:, :, None] == column[None, None, :]) & (column[None, :, None] > 0)
    reach = jnp.eye(count, dtype=jnp.float32)[None] + linked.astype(jnp.float32)
    for sweep in range(count.bit_length()):
        reach = jnp.minimum(
            jnp.einsum("gij,gjk->gik", reach, reach, precision=lax.Precision.HIGHEST), 1.0
        )
    return reach


def attend(queries, keys, values, mask):
    rows = queries.shape[0]
    length = keys.shape[0]
    kv_heads = keys.shape[1] // HEAD_SIZE
    repeats = queries.shape[1] // keys.shape[1]
    query_view = queries.reshape(rows, kv_heads, repeats, HEAD_SIZE)
    key_view = keys.reshape(length, kv_heads, HEAD_SIZE)
    value_view = values.reshape(length, kv_heads, HEAD_SIZE)
    scores = jnp.einsum(
        "qhrd,khd->hrqk", query_view, key_view, preferred_element_type=jnp.float32
    ) * HEAD_SIZE ** (-0.5)
    weights = jnp.exp(capped(scores, 50.0)) * mask[None, None]
    denominator = jnp.sum(weights, -1).transpose(2, 0, 1).reshape(rows, kv_heads * repeats)
    numerator = jnp.einsum(
        "hrqk,khd->qhrd",
        weights.astype(jnp.bfloat16),
        value_view,
        preferred_element_type=jnp.float32,
    )
    return (numerator.reshape(rows, kv_heads * repeats * HEAD_SIZE), denominator)


def per_device(
    hidden,
    medusa_w,
    embedding,
    cand_ids,
    tree_q,
    tree_key_value,
    prompt_key_value,
    block_group,
    block_len,
    block_empty,
    parents,
    out_weight,
    post_gain,
    resid,
):
    units = medusa_w.shape[2]
    inner = jnp.einsum(
        "rd,mdu->mru",
        hidden,
        lax.all_gather(medusa_w, "blk", axis=1, tiled=True),
        preferred_element_type=jnp.float32,
    )
    own_cols = lax.dynamic_slice_in_dim(hidden, lax.axis_index("mp") * units, units, 1).astype(
        jnp.float32
    )
    fresh = (own_cols[None] + jax.nn.silu(inner)).astype(jnp.bfloat16)
    full_fresh = lax.all_gather(fresh, "mp", axis=2, tiled=True)
    logits = capped(
        jnp.einsum("mrd,vd->mrv", full_fresh, embedding, preferred_element_type=jnp.float32), 30.0
    )
    totals = jnp.sum(jnp.exp(logits), -1)
    vocab_dev = embedding.shape[0]
    first_id = lax.axis_index(("blk", "mp")) * vocab_dev
    local_ids = cand_ids - first_id
    match = local_ids[..., None] == jnp.arange(vocab_dev, dtype=jnp.int32)
    picked = jnp.sum(jnp.where(match, logits[:, :, None, :], 0.0), -1)
    totals, picked = lax.psum((totals, picked), ("blk", "mp"))
    draft_logprob = picked - jnp.log(totals)[..., None]
    groups, tree_size, features = tree_q.shape
    keys = prompt_key_value[0, 0]
    values = prompt_key_value[1, 0]
    length = keys.shape[0]
    group = block_group[0]
    key_ok = ((jnp.arange(length, dtype=jnp.int32) < block_len[0]) & (block_empty[0] == 0)).astype(
        jnp.float32
    )
    row_group = jnp.arange(groups * tree_size, dtype=jnp.int32) // tree_size
    mask = (row_group == group).astype(jnp.float32)[:, None] * key_ok[None, :]
    numer, denom = attend(tree_q.reshape(groups * tree_size, features), keys, values, mask)
    rows_dev = groups * tree_size // lax.axis_size("blk")
    first_row = lax.axis_index("blk") * rows_dev
    summed = lax.psum((numer, denom), "blk")
    numer = lax.dynamic_slice_in_dim(summed[0], first_row, rows_dev, 0)
    denom = lax.dynamic_slice_in_dim(summed[1], first_row, rows_dev, 0)
    reach = ancestry(parents)
    tree_numer, tree_denom = jax.vmap(attend)(tree_q, tree_key_value[0], tree_key_value[1], reach)
    heads_dev = tree_denom.shape[2]
    tree_numer = lax.dynamic_slice_in_dim(
        tree_numer.reshape(groups * tree_size, features), first_row, rows_dev, 0
    )
    tree_denom = lax.dynamic_slice_in_dim(
        tree_denom.reshape(groups * tree_size, heads_dev), first_row, rows_dev, 0
    )
    numer = numer + tree_numer
    denom = denom + tree_denom
    heads_out = (
        (numer.reshape(rows_dev, heads_dev, HEAD_SIZE) / denom[..., None])
        .reshape(rows_dev, features)
        .astype(jnp.bfloat16)
    )
    attn = lax.psum(jnp.dot(heads_out, out_weight, preferred_element_type=jnp.float32), "mp")
    normed = attn * lax.rsqrt(jnp.mean(attn * attn, -1, keepdims=True) + 1e-06) * post_gain
    layer_out = (normed + resid.astype(jnp.float32)).astype(jnp.bfloat16)
    return (draft_logprob, layer_out)


def solution(mesh):
    placed = (
        P(),
        P(None, "blk", "mp"),
        P(("blk", "mp"), None),
        P(),
        P(None, None, "mp"),
        P(None, None, None, "mp"),
        P(None, "blk", None, "mp"),
        P("blk"),
        P("blk"),
        P("blk"),
        P(),
        P("mp", None),
        P(),
        P("blk", None),
    )
    return jax.shard_map(
        per_device, mesh=mesh, in_specs=placed, out_specs=(P(), P("blk", None)), check_vma=False
    )
```

profile of v0, /device:TPU:1, one launch (start us, length us, event | category | flops | bytes accessed | tf_op | source)
XLA Modules:
  0.0 381.7 jit_solution(4261685247920140671)
XLA Ops:
  7.2 0.0 all-reduce.4.cloned.1.call-start
  7.2 4.4 %fusion.51 = (bf16[1,1,2048,512]{3,2,1,0:T(8,128)(2,1)}, bf16[1,1,2048,512]{3,2,1,0:T(8,128)(2,1)}) fusion(bf16[2,1,2048,512]{3,2,1,0:T(8,128)(2,1)} %param.20), kind=kLoop, calls=%fused_computation.70 | loop fusion | bytes 8388608 | tf_op jit(solution)/shard_map/slice | solution.py:88
  11.6 2.9 copy.79
  16.5 3.3 reshape_reshape.3
  19.8 4.0 %copy.80 = bf16[1,1,2048,512]{2,3,1,0:T(8,128)(2,1)} copy(bf16[1,1,2048,512]{3,2,1,0:T(8,128)(2,1)} %get-tuple-element.6) | data formatting | bytes 4194304
  23.8 0.4 broadcast_multiply_fusion
  24.2 10.5 %fusion = (f32[2,2,576]{2,1,0:T(2,128)}, f32[2,2048,576,2]{1,2,3,0:T(8,128)}) fusion(f32[576,2048]{1,0:T(8,128)S(1)} %broadcast_multiply_fusion, bf16[2048,2,256,1]{0,2,3,1:T(8,128)(2,1)S(1)} %bitcast.83, bf16[576,2,2,256]{3,2,1,0:T(2,128)(2,1)S(1)} %reshape_reshape.3), kind=kOutput, calls=%fused_computation.1 | convolution fusion | flops 2434791168 | bytes 26878976 | tf_op jit(solution)/shard_map/qhrd,khd->hrqk/dot_general | solution.py:33
  34.7 9.1 %fusion.6 = f32[576,2,2,256]{3,0,2,1:T(8,128)S(1)} fusion(bf16[2048,2,256,1]{0,2,3,1:T(8,128)(2,1)S(1)} %bitcast.85, f32[2,2048,576,2]{1,2,3,0:T(8,128)} %get-tuple-element.15, f32[576,2048]{1,0:T(8,128)S(1)} %broadcast_multiply_fusion), kind=kOutput, calls=%fused_computation.10 | convolution fusion | flops 2434793472 | bytes 28049408 | tf_op jit(solution)/shard_map/hrqk,khd->qhrd/dot_general | solution.py:38
  43.8 1.8 copy.56
  45.6 2.9 reshape.101
  48.6 0.0 all-gather.3.cloned.1.call-start
  48.6 0.7 all-gather.3.cloned.1.call-update
  49.3 0.2 all-reduce.6.cloned.1.call-start
  49.6 0.3 copy-done
  49.8 0.9 reshape.102
  50.7 0.7 reshape.104
  51.4 0.1 fusion.52
  51.5 0.1 reshape_squeeze.14
  51.7 1.4 convolution_minimum_fusion.5
  53.1 0.4 convolution_minimum_fusion.4
  53.5 0.4 convolution_minimum_fusion.3
  53.9 0.4 convolution_minimum_fusion.2
  54.4 0.4 convolution_minimum_fusion.1
  54.8 0.4 convolution_minimum_fusion
  55.2 0.1 copy.59
  55.3 0.9 fusion.53
  56.2 0.1 reshape.105
  56.3 124.9 %psum.38 = f32[576,4]{0,1:T(4,128)S(1)} all-reduce(f32[576,4]{0,1:T(4,128)S(1)} %reshape.104), channel_id=1, replica_groups=mesh['blk'=32,'mp'=4] {'blk'}, use_global_device_ids=true, to_apply=%region_6.7 | all-reduce | flops 2304 | bytes 18432 | tf_op jit(solution)/shard_map/psum | solution.py:99
  181.2 0.1 dynamic-slice_add_fusion
  181.3 0.1 copy.64
  181.4 0.1 div.48
  181.5 0.1 reshape_squeeze.15
  181.7 0.5 convolution_bitcast_fusion
  182.2 1.8 copy.62
  184.1 2.9 reshape.103
  187.0 0.0 all-reduce.4.cloned.1.call-done
  187.1 5.1 %fusion.39 = f32[18,3584]{1,0:T(8,128)} fusion(bf16[1024,3584]{1,0:T(8,128)(2,1)} %param.25, f32[18,1024]{1,0:T(8,128)S(1)} %bitcast.87, f32[576,1024]{1,0:T(8,128)} %reshape.103, s32[]{:T(128)S(6)} %select_n.25, f32[576,1024]{1,0:T(8,128)} %all-reduce.4.cloned.1.call-done), kind=kOutput, calls=%fused_computation.47 | convolution fusion | flops 132175872 | bytes 7868420 | tf_op jit(solution)/shard_map/dot_general | solution.py:118
  192.2 0.3 all-gather.5.cloned.1.call-start
  192.4 32.7 %all-gather.3.cloned.1.call-done = bf16[2,3584,896]{2,1,0:T(8,128)(2,1)} async-done(((bf16[2,112,896]{2,1,0:T(8,128)(2,1)}), bf16[2,3584,896]{2,1,0:T(8,128)(2,1)}) %all-gather.3.cloned.1.call-update) | async-done | bytes 12845072 | tf_op jit(solution)/shard_map/all_gather | solution.py:67
  225.2 7.6 %add_convert_fusion = bf16[2,144,896]{2,1,0:T(8,128)(2,1)} fusion(bf16[2,3584,896]{2,1,0:T(8,128)(2,1)} %all-gather.3.cloned.1.call-done, bf16[144,3584]{1,0:T(8,128)(2,1)S(1)} %copy-done.4, f32[144,896]{1,0:T(8,128)S(1)} %dynamic-slice_convert_fusion), kind=kOutput, calls=%fused_computation.32 | convolution fusion | flops 1851236352 | bytes 14909440 | tf_op jit(solution)/shard_map/rd,mdu->mru/dot_general | solution.py:64
  232.8 34.1 %all-reduce.6.cloned.1.call-done = f32[18,3584]{1,0:T(8,128)} async-done(((f32[18,3584]{1,0:T(8,128)}), f32[18,3584]{1,0:T(8,128)}) %all-reduce.6.cloned.1.call-update) | async-done | bytes 258064 | tf_op jit(solution)/shard_map/psum | solution.py:118
  266.9 1.1 multiply_reduce_fusion
  268.0 1.8 add_convert_fusion.1
  269.8 31.7 %all-gather.5.cloned.1.call-done = bf16[2,144,3584]{2,1,0:T(8,128)(2,1)} async-done(((bf16[2,144,896]{2,1,0:T(8,128)(2,1)}), bf16[2,144,3584]{2,1,0:T(8,128)(2,1)}) %all-gather.5.cloned.1.call-update) | async-done | bytes 2064400 | tf_op jit(solution)/shard_map/all_gather | solution.py:74
  301.5 6.2 %exponential_reduce_fusion = (f32[2,144]{1,0:T(2,128)S(1)}, f32[2,144,1024]{2,1,0:T(8,128)S(1)}) fusion(bf16[2,144,3584]{2,1,0:T(8,128)(2,1)} %all-gather.5.cloned.1.call-done, bf16[1024,3584]{1,0:T(8,128)(2,1)} %param.16), kind=kOutput, calls=%fused_computation.24 | convolution fusion | flops 2114813696 | bytes 10585216 | tf_op jit(solution)/shard_map/mrd,vd->mrv/dot_general | solution.py:76
  307.8 1.8 select_reduce_fusion
  309.6 64.9 %all-reduce = (f32[2,144,10]{1,2,0:T(8,128)S(1)}, f32[2,144]{1,0:T(2,128)S(1)}) all-reduce(f32[2,144,10]{1,2,0:T(8,128)S(1)} %select_reduce_fusion, f32[2,144]{1,0:T(2,128)S(1)} %get-tuple-element.10), channel_id=1, replica_groups=mesh['blk'=32,'mp'=4] {'blk','mp'}, use_global_device_ids=true, to_apply=%region_1.2 | all-reduce | flops 3168 | bytes 25344 | tf_op jit(solution)/shard_map/psum | solution.py:84
  374.5 0.6 copy.65
  (29 shorter events, 0.2 us)
Async XLA Ops:
  7.2 179.9 %all-reduce.4.cloned.1.call-start = ((), (), s32[]{:S(2)}) async-start(), calls=%async_computation.2 | async-start | bytes 4718592 | tf_op jit(solution)/shard_map/psum | solution.py:99
  24.2 10.5 %copy-start.1 = (bf16[1,1,2048,512]{2,3,1,0:T(8,128)(2,1)S(1)}, bf16[1,1,2048,512]{2,3,1,0:T(8,128)(2,1)}, u32[]{:S(2)}) copy-start(bf16[1,1,2048,512]{2,3,1,0:T(8,128)(2,1)} %copy.80) | copy-start | bytes 6291460
  48.6 1.3 copy-start
  48.6 2.9 copy-start.2
  48.6 176.6 %all-gather.3.cloned.1.call-start = ((), (), s32[]{:S(2)}) async-start(), calls=%async_computation | async-start | bytes 13246464 | tf_op jit(solution)/shard_map/all_gather | solution.py:67
  49.3 217.6 %all-reduce.6.cloned.1.call-start = ((), (), s32[]{:S(2)}) async-start(), calls=%async_computation.3 | async-start | bytes 688128 | tf_op jit(solution)/shard_map/psum | solution.py:118
  184.0 3.0 copy-start.4
  192.1 40.7 %copy-start.5 = (s32[2,144,10]{1,0,2:T(2,128)S(1)}, s32[2,144,10]{1,0,2:T(2,128)}, u32[]{:S(2)}) copy-start(s32[2,144,10]{1,0,2:T(2,128)} %param.17) | copy-start | bytes 34564
  192.2 75.9 %copy-start.3 = (bf16[18,3584]{1,0:T(8,128)(2,1)S(1)}, bf16[18,3584]{1,0:T(8,128)(2,1)}, u32[]{:S(2)}) copy-start(bf16[18,3584]{1,0:T(8,128)(2,1)} %param.27) | copy-start | bytes 387076
  192.2 75.9 %copy-start.6 = (f32[3584]{0:T(1024)S(1)}, f32[3584]{0:T(1024)}, u32[]{:S(2)}) copy-start(f32[3584]{0:T(1024)} %param.26) | copy-start | bytes 43012
  192.2 109.4 %all-gather.5.cloned.1.call-start = ((), (), s32[]{:S(2)}) async-start(), calls=%async_computation.1 | async-start | bytes 2580480 | tf_op jit(solution)/shard_map/all_gather | solution.py:74
Sparse Core Ops, SparseCore 0:
  48.7 110.4 all-reduce.3
  161.6 63.5 all-gather.2
  227.5 39.3 all-reduce.5
  268.4 33.0 all-gather.4
where the time goes:
time: 382 us
  blocking collectives  190 us (50%)
  waiting for transfers between devices  99.3 us (26%)
  matrix products  43.3 us (11%)
  local copies, waits for them, and re-layouts  27.5 us (7%)
  between operations  16 us (4%)
  other arithmetic  5.25 us (1%)
    psum x1, blocking collectives, per_device(): summed = lax.psum((numer, denom), 'blk')  125 us
    psum x1, blocking collectives, per_device(): totals, picked = lax.psum((totals, picked), ('blk', 'mp'))  64.9 us
    psum x1, waiting for transfers between devices, per_device(): lax.psum(jnp.dot(heads_out, out_weight, preferred_element_type=jnp.float3...  34.1 us
    all_gather x1, waiting for transfers between devices, per_device(): lax.all_gather(medusa_w, 'blk', axis=1, tiled=True)  32.7 us
    all_gather x1, waiting for transfers between devices, per_device(): full_fresh = lax.all_gather(fresh, 'mp', axis=2, tiled=True)  31.7 us
    dot_general x2, matrix products, attend(): jnp.einsum('qhrd,khd->hrqk', query_view, key_view, preferred_element_type...  11.3 us
    dot_general x2, matrix products, attend(): jnp.einsum('hrqk,khd->qhrd', weights.astype(jnp.bfloat16), value_view, pr...  9.63 us
    unnamed x19, local copies, waits for them, and re-layouts  7.84 us
  transfers between devices with their start and end apart: 4, of which 3 were waited for; matrix products, arithmetic and copies ran while one was open for 7% of the time, Pallas kernels for 0%

commit v1 on v0

v1 whole, which is shorter than its diff:
```python
import jax
import jax.numpy as jnp
from jax import lax
from jax.experimental import pallas as pl
from jax.experimental.pallas import tpu as pltpu
from jax.sharding import PartitionSpec as P

MESH = pl.DeviceIdType.MESH
F32 = jnp.float32
BF16 = jnp.bfloat16

D = 3584
ROWS = 144
MROWS = 288
UNITS = 896
DEPTH = 112
GROUPS = 12
TREE = 48
HEAD = 256
HEADS = 4
SLOTS = 2048
VOCAB = 1024
TOPC = 10
NB = 32
OWNERS = (0, 11, 22)
KEY_TILE = 512
NT = (((1,), (1,)), ((), ()))
NN = (((1,), (0,)), ((), ()))


def dot(a, b, dims=NN):
    return lax.dot_general(a, b, dims, preferred_element_type=F32)


def iota(shape, axis):
    return lax.broadcasted_iota(jnp.int32, shape, axis)


def weigh(scores):
    return jnp.exp(50.0 * jnp.tanh(scores * (HEAD ** (-0.5) / 50.0)))


SCRATCH = (
    ("hwin", pltpu.VMEM((ROWS, 256), BF16)),
    ("wpad", pltpu.VMEM((2, 256, UNITS), BF16)),
    ("hown", pltpu.VMEM((2, 32, 128), BF16)),
    ("embv", pltpu.VMEM((VOCAB, D), BF16)),
    ("outv", pltpu.VMEM((HEADS * HEAD, D), BF16)),
    ("kbuf", pltpu.VMEM((SLOTS, 512), BF16)),
    ("vbuf", pltpu.VMEM((SLOTS, 512), BF16)),
    ("qbuf", pltpu.VMEM((GROUPS, TREE, 1024), BF16)),
    ("tqb", pltpu.VMEM((GROUPS, 64, HEAD), BF16)),
    ("tkb", pltpu.VMEM((GROUPS, 64, HEAD), BF16)),
    ("tvb", pltpu.VMEM((GROUPS, 64, HEAD), BF16)),
    ("candv", pltpu.VMEM((2, ROWS, TOPC), jnp.int32)),
    ("parv", pltpu.VMEM((GROUPS, TREE), jnp.int32)),
    ("gainv", pltpu.VMEM((1, D), F32)),
    ("residv", pltpu.VMEM((18, D), BF16)),
    ("sem_in", pltpu.SemaphoreType.DMA((20,))),
    ("pbuf", pltpu.VMEM((64, 32, 128), BF16)),
    ("precv", pltpu.VMEM((NB - 1, 2, 32, 128), BF16)),
    ("ps", pltpu.SemaphoreType.DMA),
    ("pr", pltpu.SemaphoreType.DMA),
    ("f0", pltpu.VMEM((4, 2, 4, 4, 32, 128), BF16)),
    ("f1", pltpu.VMEM((4, 2, 4, 4, 32, 128), BF16)),
    ("fz_s", pltpu.SemaphoreType.DMA((2,))),
    ("fz_r", pltpu.SemaphoreType.DMA((2,))),
    ("fa_s", pltpu.SemaphoreType.DMA((2,))),
    ("fa_r", pltpu.SemaphoreType.DMA((2,))),
    ("fb_s", pltpu.SemaphoreType.DMA((2,))),
    ("fb_r", pltpu.SemaphoreType.DMA((2, 3))),
    ("fc_s", pltpu.SemaphoreType.DMA((2,))),
    ("fc_r", pltpu.SemaphoreType.DMA((2,))),
    ("fresh", pltpu.VMEM((MROWS, D), BF16)),
    ("abuf", pltpu.VMEM((NB, 8, 384), BF16)),
    ("arecv", pltpu.VMEM((NB, 8, 384), BF16)),
    ("as_", pltpu.SemaphoreType.DMA),
    ("ar", pltpu.SemaphoreType.DMA),
    ("treen", pltpu.VMEM((GROUPS, 8, HEAD), F32)),
    ("treed", pltpu.VMEM((GROUPS, 8, 128), F32)),
    ("hbuf", pltpu.VMEM((GROUPS, 8, HEAD), BF16)),
    ("hrecv", pltpu.VMEM((GROUPS, 8, HEAD), BF16)),
    ("hs", pltpu.SemaphoreType.DMA((GROUPS,))),
    ("hr", pltpu.SemaphoreType.DMA),
    ("zbuf", pltpu.VMEM((4, 3, 8, D), BF16)),
    ("zs", pltpu.SemaphoreType.DMA),
    ("zr", pltpu.SemaphoreType.DMA),
    ("nrm", pltpu.VMEM((24, D), F32)),
    ("idv", pltpu.VMEM((384, 128), F32)),
    ("sbuf", pltpu.VMEM((4, 16, 384), F32)),
    ("ss", pltpu.SemaphoreType.DMA),
    ("sr", pltpu.SemaphoreType.DMA),
    ("sown", pltpu.VMEM((3, 16, 128), F32)),
    ("grecv", pltpu.VMEM((NB, 16, 128), F32)),
    ("gs", pltpu.SemaphoreType.DMA((3,))),
    ("gr", pltpu.SemaphoreType.DMA),
    ("rbuf", pltpu.VMEM((3, 16, 128), F32)),
    ("rs", pltpu.SemaphoreType.DMA),
    ("rr", pltpu.SemaphoreType.DMA((3,))),
)


class Refs:
    pass


def kernel(
    hidden, medusa_w, embedding, cand_ids, tree_q, tree_kv, prompt_kv,
    block_group, block_len, block_empty, parents, out_weight, post_gain, resid,
    out_ref, stat_ref, *scratch
):
    s = Refs()
    for (name, _), ref in zip(SCRATCH, scratch):
        setattr(s, name, ref)
    me = lax.axis_index("blk")
    mz = lax.axis_index("mp")
    mx, my, mc = me // 8, (me // 2) % 4, me % 2
    head, part = me // 8, me % 8

    def peer_of(step):
        return lax.rem(me + step, NB)

    def z_of(step):
        return lax.rem(mz + step, 4)

    def remote(src, dst, ss, rs, **where):
        return pltpu.make_async_remote_copy(
            src_ref=src, dst_ref=dst, send_sem=ss, recv_sem=rs,
            device_id=where, device_id_type=MESH,
        )

    def drain(ref, sem):
        pltpu.make_async_copy(ref, ref, sem).wait()

    inputs = []

    def fetch(src, dst):
        copy = pltpu.make_async_copy(src, dst, s.sem_in.at[len(inputs)])
        copy.start()
        inputs.append(copy)
        return copy

    first = DEPTH * me
    start = jnp.minimum((first // 128) * 128, D - 256)
    start = pl.multiple_of(start, 128)
    shift = pl.multiple_of(first - start, 16)
    for m in range(2):
        s.wpad[m] = jnp.zeros((256, UNITS), BF16)
    in_w = [
        fetch(hidden.at[:, pl.ds(start, 256)], s.hwin),
        fetch(medusa_w.at[0], s.wpad.at[0, pl.ds(shift, DEPTH), :]),
        fetch(medusa_w.at[1], s.wpad.at[1, pl.ds(shift, DEPTH), :]),
    ]
    in_q = fetch(tree_q, s.qbuf)
    in_k = fetch(prompt_kv.at[0, 0], s.kbuf)
    in_v = fetch(prompt_kv.at[1, 0], s.vbuf)
    in_h = []
    for p in range(2):
        chunk = 2 * me + p
        rblk, lane = chunk // 7, chunk % 7
        col = pl.multiple_of(mz * UNITS + lane * 128, 128)
        for half in range(2):
            row = pl.multiple_of(((rblk * 2 + half) % 9) * 16, 16)
            in_h.append(
                fetch(
                    hidden.at[pl.ds(row, 16), pl.ds(col, 128)],
                    s.hown.at[p, pl.ds(half * 16, 16), :],
                )
            )
    qcol = pl.multiple_of(head * HEAD, HEAD)
    kcol = pl.multiple_of((head // 2) * HEAD, HEAD)
    in_t = [
        fetch(tree_q.at[:, :, pl.ds(qcol, HEAD)], s.tqb.at[:, pl.ds(0, TREE), :]),
        fetch(tree_kv.at[0, :, :, pl.ds(kcol, HEAD)], s.tkb.at[:, pl.ds(0, TREE), :]),
        fetch(tree_kv.at[1, :, :, pl.ds(kcol, HEAD)], s.tvb.at[:, pl.ds(0, TREE), :]),
        fetch(parents, s.parv),
    ]
    in_c = fetch(cand_ids, s.candv)
    in_o = fetch(out_weight, s.outv)
    in_g = [fetch(post_gain, s.gainv), fetch(resid, s.residv)]
    in_e = fetch(embedding, s.embv)

    barrier = pltpu.get_barrier_semaphore()

    def greet(step, carry):
        pl.semaphore_signal(
            barrier, inc=1, device_id={"blk": peer_of(step)}, device_id_type=MESH
        )
        return carry

    lax.fori_loop(1, NB, greet, 0)
    for step in range(1, 4):
        pl.semaphore_signal(
            barrier, inc=1, device_id={"mp": z_of(step)}, device_id_type=MESH
        )

    for copy in in_w:
        copy.wait()
    hwin = s.hwin[...]
    for m in range(2):
        product = dot(hwin, s.wpad[m]).astype(BF16)
        for u in range(9):
            unit = m * 9 + u
            for lane in range(7):
                s.pbuf[(unit // 2) * 7 + lane, (unit % 2) * 16:(unit % 2) * 16 + 16, :] = (
                    product[u * 16:u * 16 + 16, lane * 128:lane * 128 + 128]
                )
    s.pbuf[63] = jnp.zeros((32, 128), BF16)
    pl.semaphore_wait(barrier, NB - 1 + 3)

    def send_product(step, carry):
        peer = peer_of(step)
        remote(
            s.pbuf.at[pl.ds(2 * peer, 2)], s.precv.at[step - 1], s.ps, s.pr, blk=peer
        ).start()
        return carry

    lax.fori_loop(1, NB, send_product, 0)

    group = block_group[0]
    limit = jnp.where(block_empty[0] == 0, block_len[0], 0)
    spread = (
        (iota((64, TREE), 0) // 8) * 6 + iota((64, TREE), 0) % 8 == iota((64, TREE), 1)
    ) & (iota((64, TREE), 0) % 8 < 6)
    spread = spread.astype(F32).astype(BF16)
    in_q.wait()
    queries = dot(spread, s.qbuf[group]).astype(BF16)
    in_k.wait()
    in_v.wait()
    row8 = iota((8, 384), 0)
    lane8 = iota((8, 384), 1)
    tag = jnp.full((8, 384), group, jnp.int32).astype(F32)
    for kv in range(2):
        cols = slice(kv * HEAD, kv * HEAD + HEAD)
        two = jnp.concatenate(
            [queries[:, (2 * kv + r) * HEAD:(2 * kv + r + 1) * HEAD] for r in range(2)], 0
        )
        numer = jnp.zeros((128, HEAD), F32)
        denom = jnp.zeros((128, 128), F32)
        for tile in range(SLOTS // KEY_TILE):
            keys = slice(tile * KEY_TILE, tile * KEY_TILE + KEY_TILE)
            seen = iota((128, KEY_TILE), 1) + tile * KEY_TILE < limit
            weight = jnp.where(seen, weigh(dot(two, s.kbuf[keys, cols], NT)), 0.0)
            for piece in range(KEY_TILE // 128):
                denom = denom + weight[:, piece * 128:piece * 128 + 128]
            numer = numer + dot(weight.astype(BF16), s.vbuf[keys, cols])
        total = jnp.broadcast_to(jnp.sum(denom, 1, keepdims=True), (128, 128))
        high = total.astype(BF16).astype(F32)
        pair = jnp.where(iota((128, 128), 1) < 64, high, total - high)
        both = jnp.concatenate([numer, pair], 1)
        for r in range(2):
            for q in range(8):
                rows = both[r * 64 + q * 8:r * 64 + q * 8 + 8]
                s.abuf[(2 * kv + r) * 8 + q] = jnp.where(row8 < 6, rows, tag).astype(BF16)

    def send_attention(step, carry):
        peer = peer_of(step)
        remote(s.abuf.at[peer], s.arecv.at[step], s.as_, s.ar, blk=peer).start()
        return carry

    lax.fori_loop(1, NB, send_attention, 0)
    s.arecv[0] = s.abuf[me]

    for copy in in_h:
        copy.wait()
    drain(s.precv, s.pr)
    inner = lax.fori_loop(
        0, NB - 1,
        lambda i, acc: acc + s.precv[i].astype(F32),
        s.pbuf[pl.ds(2 * me, 2)].astype(F32),
    )
    fresh = (s.hown[...].astype(F32) + inner / (1.0 + jnp.exp(-inner))).astype(BF16)
    s.f0[my, mc, mx, mz] = fresh[0]
    s.f1[mx, mc, my, mz] = fresh[1]
    for step in range(1, 4):
        for which, own in enumerate((s.f0.at[my, mc, mx, mz], s.f1.at[mx, mc, my, mz])):
            remote(own, own, s.fz_s.at[which], s.fz_r.at[which], mp=z_of(step)).start()

    for copy in in_t:
        copy.wait()
    for buf in (s.tqb, s.tkb, s.tvb):
        for g in range(GROUPS):
            buf[g, TREE:64, :] = jnp.zeros((64 - TREE, HEAD), BF16)
    place = (iota((TREE, 256), 0) == iota((TREE, 256), 1) % 64).astype(F32).astype(BF16)
    spots = dot(s.parv[...].astype(F32).astype(BF16), place)
    sub = iota((256, 256), 0)
    lan = iota((256, 256), 1)
    eye = sub == lan
    pick_row = iota((32, 256), 0)
    pick_col = iota((32, 256), 1)
    pick = (pick_col == (pick_row // 8) * 64 + part * 6 + pick_row % 8) & (pick_row % 8 < 6)
    pick = pick.astype(F32).astype(BF16)
    for b in range(3):
        mine = iota((GROUPS, 256), 0) == 4 * b + iota((GROUPS, 256), 1) // 64
        parent = jnp.sum(jnp.where(mine, spots, 0.0), 0, keepdims=True)
        wanted = parent + (iota((1, 256), 1) // 64 * 64).astype(F32)
        linked = (sub.astype(F32) == wanted) & (lan % 64 > 0)
        reach = jnp.where(eye | linked, 1.0, 0.0).astype(BF16)
        for sweep in range(6):
            reach = jnp.minimum(dot(reach, reach), 1.0).astype(BF16)
        mask = dot(pick, reach, NT)
        tq = s.tqb[4 * b:4 * b + 4].reshape(256, HEAD)
        tk = s.tkb[4 * b:4 * b + 4].reshape(256, HEAD)
        tv = s.tvb[4 * b:4 * b + 4].reshape(256, HEAD)
        rows = dot(pick, tq).astype(BF16)
        weight = weigh(dot(rows, tk, NT)) * mask
        numer = dot(weight.astype(BF16), tv)
        denom = jnp.broadcast_to(jnp.sum(weight, 1, keepdims=True), (32, 128))
        s.treen[4 * b:4 * b + 4] = numer.reshape(4, 8, HEAD)
        s.treed[4 * b:4 * b + 4] = denom.reshape(4, 8, 128)

    def x_peer(step):
        return lax.rem(mx + step, 4) * 8 + my * 2 + mc

    def y_peer(step):
        return mx * 8 + lax.rem(my + step, 4) * 2 + mc

    lines = ((s.f0, my, mx, x_peer, y_peer), (s.f1, mx, my, y_peer, x_peer))
    for which, (buf, slow, quick, near, far) in enumerate(lines):
        drain(buf.at[slow, mc, quick, pl.ds(0, 3)], s.fz_r.at[which])
        own = buf.at[slow, mc, quick]
        for step in range(1, 4):
            remote(own, own, s.fa_s.at[which], s.fa_r.at[which], blk=near(step)).start()

    drain(s.arecv.at[pl.ds(1, NB - 1)], s.ar)
    for half in range(2):
        def add(i, carry):
            got = s.arecv[i].astype(F32)
            named = jnp.broadcast_to(got[6:7], (8, 384))
            return tuple(
                acc + jnp.where(named == float(half * 6 + g), got, 0.0)
                for g, acc in enumerate(carry)
            )

        sums = lax.fori_loop(0, NB, add, (jnp.zeros((8, 384), F32),) * 6)
        for g in range(6):
            both = sums[g]
            pair = both[:, HEAD:]
            denom = pair[:, :1] + pair[:, 64:65] + s.treed[half * 6 + g][:, :1]
            denom = jnp.where(iota((8, 1), 0) < 6, denom, 1.0)
            numer = both[:, :HEAD] + s.treen[half * 6 + g]
            numer = jnp.where(iota((8, HEAD), 0) < 6, numer, 0.0)
            s.hbuf[half * 6 + g] = (numer / denom).astype(BF16)

    def heads_copy(g):
        chunk = g * 8 + part
        owner = chunk // 3
        spot = (chunk % 3) * 4 + head
        return owner, spot

    def send_heads(g, carry):
        owner, spot = heads_copy(g)

        @pl.when(owner != me)
        def _():
            remote(
                s.hbuf.at[g], s.hrecv.at[spot], s.hs.at[g], s.hr, blk=owner
            ).start()

        @pl.when(owner == me)
        def _():
            pltpu.make_async_copy(s.hbuf.at[g], s.hrecv.at[spot], s.hr).start()

        return carry

    lax.fori_loop(0, GROUPS, send_heads, 0)

    sibling = me + 1 - 2 * mc
    for which, (buf, slow, quick, near, far) in enumerate(lines):
        drain(buf.at[slow, mc, pl.ds(0, 3)], s.fa_r.at[which])
        own = buf.at[slow, mc]
        for step in range(1, 4):
            remote(own, own, s.fb_s.at[which], s.fb_r.at[which, step - 1], blk=far(step)).start()
        remote(own, own, s.fc_s.at[which], s.fc_r.at[which], blk=sibling).start()

    in_o.wait()
    drain(s.hrecv, s.hr)
    lhs = jnp.concatenate(
        [
            jnp.concatenate([s.hrecv[t * 4 + h].astype(F32) for h in range(HEADS)], 1)
            for t in range(3)
        ],
        0,
    ).astype(BF16)
    for tile in range(7):
        cols = slice(tile * 512, tile * 512 + 512)
        got = dot(lhs, s.outv[:, cols]).astype(BF16)
        s.zbuf[mz, :, :, cols] = got.reshape(3, 8, 512)
    for step in range(1, 4):
        own = s.zbuf.at[mz]
        remote(own, own, s.zs, s.zr, mp=z_of(step)).start()

    in_c.wait()
    s.idv[...] = jnp.zeros((384, 128), F32)
    for m in range(2):
        s.idv[m * ROWS:m * ROWS + ROWS, 0:TOPC] = s.candv[m].astype(F32)
    ids = s.idv[...].T
    base = ((me * 4 + mz) * VOCAB).astype(F32)

    for step in range(1, 4):
        for which, (buf, slow, quick, near, far) in enumerate(lines):
            came = buf.at[lax.rem(slow - step + 4, 4), mc]
            drain(came, s.fb_r.at[which, step - 1])
            remote(came, came, s.fc_s.at[which], s.fc_r.at[which], blk=sibling).start()
    for which, (buf, slow, quick, near, far) in enumerate(lines):
        drain(buf.at[pl.ds(0, 2)], s.fc_r.at[which])

    def arrange(owner, carry):
        x, y, c = owner // 8, (owner // 2) % 4, owner % 2
        for p in range(2):
            chunk = 2 * owner + p
            row = pl.multiple_of((chunk // 7) * 32, 32)

            @pl.when(chunk < 63)
            def _():
                for z in range(4):
                    col = pl.multiple_of(z * UNITS + (chunk % 7) * 128, 128)
                    piece = s.f0[y, c, x, z] if p == 0 else s.f1[x, c, y, z]
                    s.fresh[pl.ds(row, 32), pl.ds(col, 128)] = piece

        return carry

    lax.fori_loop(0, NB, arrange, 0)

    in_e.wait()
    tall = iota((16, MROWS), 0)

    def score(tile, acc):
        rows = pl.multiple_of(tile * 256, 256)
        raw = dot(s.embv[pl.ds(rows, 256), :], s.fresh[...], NT)
        logits = 30.0 * jnp.tanh(raw * (1.0 / 30.0))
        acc = acc + jnp.where(tall == 0, jnp.sum(jnp.exp(logits), 0, keepdims=True), 0.0)
        here = (iota((256, MROWS), 0) + tile * 256).astype(F32) + base
        for c in range(TOPC):
            chosen = jnp.where(here == ids[c:c + 1, :MROWS], logits, 0.0)
            acc = acc + jnp.where(tall == c + 1, jnp.sum(chosen, 0, keepdims=True), 0.0)
        return acc

    stats = lax.fori_loop(0, 4, score, jnp.zeros((16, MROWS), F32))
    s.sbuf[mz] = jnp.concatenate([stats, jnp.zeros((16, 384 - MROWS), F32)], 1)
    for step in range(1, 4):
        own = s.sbuf.at[mz]
        remote(own, own, s.ss, s.sr, mp=z_of(step)).start()

    for copy in in_g:
        copy.wait()
    drain(s.zbuf.at[pl.ds(0, 3)], s.zr)
    attn = s.zbuf[0].astype(F32)
    for z in range(1, 4):
        attn = attn + s.zbuf[z].astype(F32)
    mean = jnp.sum(attn * attn, -1, keepdims=True) * (1.0 / D)
    normed = attn * lax.rsqrt(mean + 1e-06) * s.gainv[...][None]
    for t in range(3):
        s.nrm[6 * t:6 * t + 6, :] = normed[t, :6]
    out_ref[...] = (s.nrm[0:18, :] + s.residv[...].astype(F32)).astype(BF16)

    drain(s.sbuf.at[pl.ds(0, 3)], s.sr)
    summed = s.sbuf[0] + s.sbuf[1] + s.sbuf[2] + s.sbuf[3]
    for t in range(3):
        s.sown[t] = summed[:, t * 128:t * 128 + 128]
    for t in range(3):
        @pl.when(me != OWNERS[t])
        def _():
            remote(
                s.sown.at[t], s.grecv.at[me], s.gs.at[t], s.gr, blk=OWNERS[t]
            ).start()

    for t in range(3):
        @pl.when(me == OWNERS[t])
        def _():
            s.grecv[OWNERS[t]] = s.sown[t]
            drain(s.grecv.at[pl.ds(0, NB - 1)], s.gr)
            full = lax.fori_loop(
                1, NB, lambda i, acc: acc + s.grecv[i], s.grecv[0]
            )
            s.rbuf[t] = full - jnp.log(full[0:1])

            def tell(step, carry):
                remote(
                    s.rbuf.at[t], s.rbuf.at[t], s.rs, s.rr.at[t], blk=peer_of(step)
                ).start()
                return carry

            lax.fori_loop(1, NB, tell, 0)
            drain(s.grecv.at[pl.ds(0, NB - 1)], s.rs)

    for t in range(3):
        @pl.when(me != OWNERS[t])
        def _():
            drain(s.rbuf.at[t], s.rr.at[t])
            drain(s.sown.at[t], s.gs.at[t])

    stat_ref[...] = s.rbuf[...]

    drain(s.precv, s.ps)
    drain(s.arecv.at[pl.ds(1, NB - 1)], s.as_)
    for which, (buf, slow, quick, near, far) in enumerate(lines):
        drain(buf.at[slow, mc, quick, pl.ds(0, 3)], s.fz_s.at[which])
        drain(buf.at[slow, mc, pl.ds(0, 3)], s.fa_s.at[which])
        drain(buf.at[pl.ds(0, 3), mc], s.fb_s.at[which])
        drain(buf.at[pl.ds(0, 2)], s.fc_s.at[which])

    def sent_heads(g, carry):
        owner, spot = heads_copy(g)

        @pl.when(owner != me)
        def _():
            drain(s.hbuf.at[g], s.hs.at[g])

        return carry

    lax.fori_loop(0, GROUPS, sent_heads, 0)
    drain(s.zbuf.at[pl.ds(0, 3)], s.zs)
    drain(s.sbuf.at[pl.ds(0, 3)], s.ss)


def per_device(
    hidden, medusa_w, embedding, cand_ids, tree_q, tree_key_value, prompt_key_value,
    block_group, block_len, block_empty, parents, out_weight, post_gain, resid,
):
    anywhere = pl.BlockSpec(memory_space=pl.ANY)
    scalar = pl.BlockSpec(memory_space=pltpu.SMEM)
    whole = pl.BlockSpec(memory_space=pltpu.VMEM)
    layer_out, stats = pl.pallas_call(
        kernel,
        out_shape=(
            jax.ShapeDtypeStruct((18, D), BF16),
            jax.ShapeDtypeStruct((3, 16, 128), F32),
        ),
        in_specs=[anywhere] * 7 + [scalar] * 3 + [anywhere] * 4,
        out_specs=(whole, whole),
        scratch_shapes=[kind for _, kind in SCRATCH],
        compiler_params=pltpu.CompilerParams(
            collective_id=0, has_side_effects=True, vmem_limit_bytes=60 << 20
        ),
    )(
        hidden, medusa_w, embedding, cand_ids, tree_q, tree_key_value, prompt_key_value,
        block_group, block_len, block_empty, parents, out_weight,
        post_gain.reshape(1, D), resid,
    )
    picked = jnp.concatenate([stats[t, 1:1 + TOPC] for t in range(3)], 1)[:, :MROWS]
    return (picked.T.reshape(2, ROWS, TOPC), layer_out)


def solution(mesh):
    placed = (
        P(),
        P(None, "blk", "mp"),
        P(("blk", "mp"), None),
        P(),
        P(None, None, "mp"),
        P(None, None, None, "mp"),
        P(None, "blk", None, "mp"),
        P("blk"),
        P("blk"),
        P("blk"),
        P(),
        P("mp", None),
        P(),
        P("blk", None),
    )
    return jax.shard_map(
        per_device, mesh=mesh, in_specs=placed, out_specs=(P(), P("blk", None)), check_vma=False
    )
```

time: 382 us -> 70 us (0.18)
  blocking collectives: 190 us -> 0 us
  waiting for transfers between devices: 99.3 us -> 0 us
  Pallas kernels: 0 us -> 61.2 us
  matrix products: 43.3 us -> 0 us
  local copies, waits for them, and re-layouts: 27.5 us -> 5.86 us
  between operations: 16 us -> 2.58 us
  other arithmetic: 5.25 us -> 0.01 us
    psum x2 -> x0, blocking collectives: 190 us -> none  [the longest x1 125 us: per_device(): summed = lax.psum((numer, denom), 'blk')]
    all_gather x2 -> x0, waiting for transfers between devices: 64.4 us -> none  [the longest x1 32.7 us: per_device(): lax.all_gather(medusa_w, 'blk', axis=1, tiled=True)]
    pallas_call x0 -> x1, Pallas kernels: none -> 61.2 us  [per_device(): pl.pallas_call(kernel, out_shape=(jax.ShapeDtypeStruct((18, D), BF16), ja...]
    dot_general x13 -> x0, matrix products: 43.3 us -> none  [the longest x2 11.3 us: attend(): jnp.einsum('qhrd,khd->hrqk', query_view, key_view, preferred_element_type...]
    psum x2 -> x0, waiting for transfers between devices: 34.1 us -> none  [the longest x1 34.1 us: per_device(): lax.psum(jnp.dot(heads_out, out_weight, preferred_element_type=jnp.float3...]
    reshape x5 -> x2, local copies, waits for them, and re-layouts: 7.57 us -> 2.02 us  [the longest x1 1.33 us: per_device(): post_gain.reshape(1, D)]
    unnamed x19 -> x2, local copies, waits for them, and re-layouts: 7.84 us -> 3.1 us
    slice x2 -> x0, local copies, waits for them, and re-layouts: 4.5 us -> none  [the longest x1 4.42 us: per_device(): values = prompt_key_value[1, 0]]
  transfers between devices with their start and end apart: 4 -> 0, of which waited for: 3 -> 0; matrix products, arithmetic and copies ran while one was open for 7% -> 0% of each run, Pallas kernels for 0% -> 0%
where the time goes in v1:
time: 70 us; the launch traced here: 69.7 us
  Pallas kernels  61.2 us (87%)
  local copies, waits for them, and re-layouts  5.86 us (8%)
  between operations  2.58 us (4%)
    pallas_call x1, Pallas kernels, per_device(): pl.pallas_call(kernel, out_shape=(jax.ShapeDtypeStruct((18, D), BF16), ja...  61.2 us
    unnamed x2, local copies, waits for them, and re-layouts  3.1 us

profile of v1, /device:TPU:1, one launch (start us, length us, event | category | flops | bytes accessed | tf_op | source)
XLA Modules:
  0.0 69.7 jit_solution(14726362172976573895)
XLA Ops:
  2.6 1.3 %reshape.10.post_gain = f32[1,3584]{1,0:T(1,128)} reshape(f32[3584]{0:T(1024)} %param.26) | data formatting | bytes 28672 | tf_op jit(solution)/shard_map/reshape | solution.py:539
  3.9 1.5 %copy.16.cand_ids = s32[2,144,10]{2,1,0:T(8,128)} copy(s32[2,144,10]{1,0,2:T(2,128)} %param.17) | data formatting | bytes 23040 | tf_op args[3]
  5.4 61.2 %shard_map.149 = (bf16[18,3584]{1,0:T(8,128)(2,1)}, f32[3,16,128]{2,1,0:T(8,128)}) custom-call(bf16[144,3584]{1,0:T(8,128)(2,1)} %hidden.1, bf16[2,112,896]{2,1,0:T(8,128)(2,1)} %medusa_w.1, bf16[1024,3584]{1,0:T(8,128)(2,1)} %embedding.1, s32[2,144,10]{2,1,0:T(8,128)} %copy.16.cand_ids, bf16[12,48,1024]{2,1,0:T(8,128)(2,1)} %tree_q.1, ...), custom_call_target="tpu_custom_call" | custom-call | tf_op jit(solution)/shard_map/pallas_call | solution.py:524
  66.6 0.7 %slice_bitcast_fusion.2 = (f32[10,128]{1,0:T(8,128)S(1)}, f32[10,128]{1,0:T(8,128)S(1)}, f32[10,128]{1,0:T(8,128)S(1)}) fusion(f32[3,16,128]{2,1,0:T(8,128)} %get-tuple-element.4), kind=kLoop, calls=%fused_computation.5 | loop fusion | bytes 30720 | tf_op jit(solution)/shard_map/squeeze | solution.py:541
  67.4 0.7 reshape.11
  68.1 1.6 %copy.21 = bf16[18,3584]{1,0:T(8,128)(2,1)} copy(bf16[18,3584]{1,0:T(8,128)(2,1)} %get-tuple-element.12) | data formatting | bytes 258048
  (1 shorter events, 0.0 us)

commit v2 on v1

--- a/solution.py
+++ b/solution.py
@@ -22,7 +22,7 @@
 VOCAB = 1024
 TOPC = 10
 NB = 32
-OWNERS = (0, 11, 22)
+CHIPS = 16
 KEY_TILE = 512
 NT = (((1,), (1,)), ((), ()))
 NN = (((1,), (0,)), ((), ()))
@@ -52,13 +52,17 @@
     ("tqb", pltpu.VMEM((GROUPS, 64, HEAD), BF16)),
     ("tkb", pltpu.VMEM((GROUPS, 64, HEAD), BF16)),
     ("tvb", pltpu.VMEM((GROUPS, 64, HEAD), BF16)),
-    ("candv", pltpu.VMEM((2, ROWS, TOPC), jnp.int32)),
+    ("candv", pltpu.VMEM((TOPC, 2, ROWS), jnp.int32)),
     ("parv", pltpu.VMEM((GROUPS, TREE), jnp.int32)),
-    ("gainv", pltpu.VMEM((1, D), F32)),
+    ("gainv", pltpu.VMEM((D,), F32)),
     ("residv", pltpu.VMEM((18, D), BF16)),
     ("sem_in", pltpu.SemaphoreType.DMA((20,))),
-    ("pbuf", pltpu.VMEM((64, 32, 128), BF16)),
-    ("precv", pltpu.VMEM((NB - 1, 2, 32, 128), BF16)),
+    ("pbuf", pltpu.VMEM((CHIPS, 2, 2, 32, 128), BF16)),
+    ("psib", pltpu.VMEM((CHIPS, 2, 32, 128), BF16)),
+    ("psum", pltpu.VMEM((CHIPS, 2, 32, 128), BF16)),
+    ("precv", pltpu.VMEM((CHIPS - 1, 2, 32, 128), BF16)),
+    ("pc_s", pltpu.SemaphoreType.DMA),
+    ("pc_r", pltpu.SemaphoreType.DMA),
     ("ps", pltpu.SemaphoreType.DMA),
     ("pr", pltpu.SemaphoreType.DMA),
     ("f0", pltpu.VMEM((4, 2, 4, 4, 32, 128), BF16)),
@@ -66,14 +70,14 @@
     ("fz_s", pltpu.SemaphoreType.DMA((2,))),
     ("fz_r", pltpu.SemaphoreType.DMA((2,))),
     ("fa_s", pltpu.SemaphoreType.DMA((2,))),
-    ("fa_r", pltpu.SemaphoreType.DMA((2,))),
+    ("fa_r", pltpu.SemaphoreType.DMA((2, 3))),
     ("fb_s", pltpu.SemaphoreType.DMA((2,))),
     ("fb_r", pltpu.SemaphoreType.DMA((2, 3))),
     ("fc_s", pltpu.SemaphoreType.DMA((2,))),
     ("fc_r", pltpu.SemaphoreType.DMA((2,))),
     ("fresh", pltpu.VMEM((MROWS, D), BF16)),
-    ("abuf", pltpu.VMEM((NB, 8, 384), BF16)),
-    ("arecv", pltpu.VMEM((NB, 8, 384), BF16)),
+    ("abuf", pltpu.VMEM((NB, 8, HEAD), BF16)),
+    ("arecv", pltpu.VMEM((NB, 8, HEAD), BF16)),
     ("as_", pltpu.SemaphoreType.DMA),
     ("ar", pltpu.SemaphoreType.DMA),
     ("treen", pltpu.VMEM((GROUPS, 8, HEAD), F32)),
@@ -86,17 +90,16 @@
     ("zs", pltpu.SemaphoreType.DMA),
     ("zr", pltpu.SemaphoreType.DMA),
     ("nrm", pltpu.VMEM((24, D), F32)),
-    ("idv", pltpu.VMEM((384, 128), F32)),
-    ("sbuf", pltpu.VMEM((4, 16, 384), F32)),
+    ("idv", pltpu.VMEM((2, 16, 384), F32)),
+    ("idb", pltpu.VMEM((TOPC, MROWS, 128), F32)),
+    ("raw", pltpu.VMEM((MROWS, VOCAB), F32)),
+    ("cols", pltpu.VMEM((384, 128), F32)),
+    ("sbuf", pltpu.VMEM((8, 16, 384), BF16)),
     ("ss", pltpu.SemaphoreType.DMA),
     ("sr", pltpu.SemaphoreType.DMA),
-    ("sown", pltpu.VMEM((3, 16, 128), F32)),
-    ("grecv", pltpu.VMEM((NB, 16, 128), F32)),
-    ("gs", pltpu.SemaphoreType.DMA((3,))),
+    ("gbuf", pltpu.VMEM((CHIPS, 16, 384), BF16)),
+    ("gs", pltpu.SemaphoreType.DMA),
     ("gr", pltpu.SemaphoreType.DMA),
-    ("rbuf", pltpu.VMEM((3, 16, 128), F32)),
-    ("rs", pltpu.SemaphoreType.DMA),
-    ("rr", pltpu.SemaphoreType.DMA((3,))),
 )
 
 
@@ -114,11 +117,16 @@
         setattr(s, name, ref)
     me = lax.axis_index("blk")
     mz = lax.axis_index("mp")
-    mx, my, mc = me // 8, (me // 2) % 4, me % 2
+    chip, mc = me // 2, me % 2
+    mx, my = chip // 4, chip % 4
+    sibling = me + 1 - 2 * mc
     head, part = me // 8, me % 8
 
     def peer_of(step):
         return lax.rem(me + step, NB)
+
+    def chip_of(step):
+        return lax.rem(chip + step, CHIPS)
 
     def z_of(step):
         return lax.rem(mz + step, 4)
@@ -193,6 +201,9 @@
         pl.semaphore_signal(
             barrier, inc=1, device_id={"mp": z_of(step)}, device_id_type=MESH
         )
+        pl.semaphore_signal(
+            barrier, inc=1, device_id={"blk": sibling, "mp": z_of(step)}, device_id_type=MESH
+        )
 
     for copy in in_w:
         copy.wait()
@@ -202,20 +213,23 @@
         for u in range(9):
             unit = m * 9 + u
             for lane in range(7):
-                s.pbuf[(unit // 2) * 7 + lane, (unit % 2) * 16:(unit % 2) * 16 + 16, :] = (
+                chunk = (unit // 2) * 7 + lane
+                low = (unit % 2) * 16
+                s.pbuf[chunk // 4, chunk // 2 % 2, chunk % 2, low:low + 16, :] = (
                     product[u * 16:u * 16 + 16, lane * 128:lane * 128 + 128]
                 )
-    s.pbuf[63] = jnp.zeros((32, 128), BF16)
-    pl.semaphore_wait(barrier, NB - 1 + 3)
+    s.pbuf[CHIPS - 1, 1, 1] = jnp.zeros((32, 128), BF16)
+    pl.semaphore_wait(barrier, NB - 1 + 6)
+    remote(s.pbuf.at[:, 1 - mc], s.psib, s.pc_s, s.pc_r, blk=sibling).start()
+    drain(s.psib, s.pc_r)
+    s.psum[...] = (s.pbuf[:, mc].astype(F32) + s.psib[...].astype(F32)).astype(BF16)
 
     def send_product(step, carry):
-        peer = peer_of(step)
-        remote(
-            s.pbuf.at[pl.ds(2 * peer, 2)], s.precv.at[step - 1], s.ps, s.pr, blk=peer
-        ).start()
+        to = chip_of(step)
+        remote(s.psum.at[to], s.precv.at[step - 1], s.ps, s.pr, blk=2 * to + mc).start()
         return carry
 
-    lax.fori_loop(1, NB, send_product, 0)
+    lax.fori_loop(1, CHIPS, send_product, 0)
 
     group = block_group[0]
     limit = jnp.where(block_empty[0] == 0, block_len[0], 0)
@@ -227,9 +241,10 @@
     queries = dot(spread, s.qbuf[group]).astype(BF16)
     in_k.wait()
     in_v.wait()
-    row8 = iota((8, 384), 0)
-    lane8 = iota((8, 384), 1)
-    tag = jnp.full((8, 384), group, jnp.int32).astype(F32)
+    row8 = iota((8, HEAD), 0)
+    row_l = iota((8, 128), 0)
+    lane_l = iota((8, 128), 1)
+    tag = jnp.full((8, HEAD), group, jnp.int32).astype(F32)
     for kv in range(2):
         cols = slice(kv * HEAD, kv * HEAD + HEAD)
         two = jnp.concatenate(
@@ -246,12 +261,17 @@
             numer = numer + dot(weight.astype(BF16), s.vbuf[keys, cols])
         total = jnp.broadcast_to(jnp.sum(denom, 1, keepdims=True), (128, 128))
         high = total.astype(BF16).astype(F32)
-        pair = jnp.where(iota((128, 128), 1) < 64, high, total - high)
-        both = jnp.concatenate([numer, pair], 1)
+        rest = total - high
         for r in range(2):
             for q in range(8):
-                rows = both[r * 64 + q * 8:r * 64 + q * 8 + 8]
-                s.abuf[(2 * kv + r) * 8 + q] = jnp.where(row8 < 6, rows, tag).astype(BF16)
+                rows = slice(r * 64 + q * 8, r * 64 + q * 8 + 8)
+                spots = jnp.where(lane_l == row_l, high[rows], 0.0) + jnp.where(
+                    lane_l == row_l + 8, rest[rows], 0.0
+                )
+                spots = jnp.sum(jnp.where(row_l < 6, spots, 0.0), 0, keepdims=True)
+                spots = jnp.concatenate([spots, jnp.zeros((1, 128), F32)], 1)
+                piece = jnp.where(row8 < 6, numer[rows], jnp.where(row8 == 6, spots, tag))
+                s.abuf[(2 * kv + r) * 8 + q] = piece.astype(BF16)
 
     def send_attention(step, carry):
         peer = peer_of(step)
@@ -265,9 +285,9 @@
         copy.wait()
     drain(s.precv, s.pr)
     inner = lax.fori_loop(
-        0, NB - 1,
+        0, CHIPS - 1,
         lambda i, acc: acc + s.precv[i].astype(F32),
-        s.pbuf[pl.ds(2 * me, 2)].astype(F32),
+        s.psum[chip].astype(F32),
     )
     fresh = (s.hown[...].astype(F32) + inner / (1.0 + jnp.exp(-inner))).astype(BF16)
     s.f0[my, mc, mx, mz] = fresh[0]
@@ -316,30 +336,41 @@
         return mx * 8 + lax.rem(my + step, 4) * 2 + mc
 
     lines = ((s.f0, my, mx, x_peer, y_peer), (s.f1, mx, my, y_peer, x_peer))
+    def pass_on(which, block, far):
+        for step in range(1, 4):
+            remote(
+                block, block, s.fb_s.at[which], s.fb_r.at[which, step - 1], blk=far(step)
+            ).start()
+        remote(block, block, s.fc_s.at[which], s.fc_r.at[which], blk=sibling).start()
+
     for which, (buf, slow, quick, near, far) in enumerate(lines):
         drain(buf.at[slow, mc, quick, pl.ds(0, 3)], s.fz_r.at[which])
         own = buf.at[slow, mc, quick]
         for step in range(1, 4):
-            remote(own, own, s.fa_s.at[which], s.fa_r.at[which], blk=near(step)).start()
+            remote(
+                own, own, s.fa_s.at[which], s.fa_r.at[which, step - 1], blk=near(step)
+            ).start()
+    for which, (buf, slow, quick, near, far) in enumerate(lines):
+        pass_on(which, buf.at[slow, mc, quick], far)
 
     drain(s.arecv.at[pl.ds(1, NB - 1)], s.ar)
     for half in range(2):
         def add(i, carry):
             got = s.arecv[i].astype(F32)
-            named = jnp.broadcast_to(got[6:7], (8, 384))
+            named = jnp.broadcast_to(got[7:8], (8, HEAD))
             return tuple(
                 acc + jnp.where(named == float(half * 6 + g), got, 0.0)
                 for g, acc in enumerate(carry)
             )
 
-        sums = lax.fori_loop(0, NB, add, (jnp.zeros((8, 384), F32),) * 6)
+        sums = lax.fori_loop(0, NB, add, (jnp.zeros((8, HEAD), F32),) * 6)
         for g in range(6):
-            both = sums[g]
-            pair = both[:, HEAD:]
-            denom = pair[:, :1] + pair[:, 64:65] + s.treed[half * 6 + g][:, :1]
+            spots = jnp.broadcast_to(sums[g][6:7, :128], (8, 128))
+            spots = jnp.where((lane_l == row_l) | (lane_l == row_l + 8), spots, 0.0)
+            denom = jnp.sum(spots, 1, keepdims=True) + s.treed[half * 6 + g][:, :1]
             denom = jnp.where(iota((8, 1), 0) < 6, denom, 1.0)
-            numer = both[:, :HEAD] + s.treen[half * 6 + g]
-            numer = jnp.where(iota((8, HEAD), 0) < 6, numer, 0.0)
+            numer = sums[g] + s.treen[half * 6 + g]
+            numer = jnp.where(row8 < 6, numer, 0.0)
             s.hbuf[half * 6 + g] = (numer / denom).astype(BF16)
 
     def heads_copy(g):
@@ -365,13 +396,11 @@
 
     lax.fori_loop(0, GROUPS, send_heads, 0)
 
-    sibling = me + 1 - 2 * mc
-    for which, (buf, slow, quick, near, far) in enumerate(lines):
-        drain(buf.at[slow, mc, pl.ds(0, 3)], s.fa_r.at[which])
-        own = buf.at[slow, mc]
-        for step in range(1, 4):
-            remote(own, own, s.fb_s.at[which], s.fb_r.at[which, step - 1], blk=far(step)).start()
-        remote(own, own, s.fc_s.at[which], s.fc_r.at[which], blk=sibling).start()
+    for step in range(1, 4):
+        for which, (buf, slow, quick, near, far) in enumerate(lines):
+            came = buf.at[slow, mc, lax.rem(quick - step + 4, 4)]
+            drain(came, s.fa_r.at[which, step - 1])
+            pass_on(which, came, far)
 
     in_o.wait()
     drain(s.hrecv, s.hr)
@@ -391,56 +420,95 @@
         remote(own, own, s.zs, s.zr, mp=z_of(step)).start()
 
     in_c.wait()
-    s.idv[...] = jnp.zeros((384, 128), F32)
+    s.idv[...] = jnp.zeros((2, 16, 384), F32)
     for m in range(2):
-        s.idv[m * ROWS:m * ROWS + ROWS, 0:TOPC] = s.candv[m].astype(F32)
-    ids = s.idv[...].T
+        s.idv[m, 0:TOPC, 0:ROWS] = s.candv[:, m, :].astype(F32)
+    ids = s.idv[0] + pltpu.roll(s.idv[1], ROWS, 1)
     base = ((me * 4 + mz) * VOCAB).astype(F32)
+    ids = jnp.concatenate([ids - base, jnp.zeros((112, 384), F32)], 0).T
+    for c in range(TOPC):
+        s.idb[c] = jnp.broadcast_to(ids[:MROWS, c:c + 1], (MROWS, 128))
 
     for step in range(1, 4):
         for which, (buf, slow, quick, near, far) in enumerate(lines):
             came = buf.at[lax.rem(slow - step + 4, 4), mc]
             drain(came, s.fb_r.at[which, step - 1])
             remote(came, came, s.fc_s.at[which], s.fc_r.at[which], blk=sibling).start()
+
+    def arrange(core):
+        def body(one, carry):
+            x, y = one // 4, one % 4
+            for p in range(2):
+                chunk = 4 * one + 2 * core + p
+                row = pl.multiple_of((chunk // 7) * 32, 32)
+
+                @pl.when(chunk < 63)
+                def _():
+                    for z in range(4):
+                        col = pl.multiple_of(z * UNITS + (chunk % 7) * 128, 128)
+                        piece = s.f0[y, core, x, z] if p == 0 else s.f1[x, core, y, z]
+                        s.fresh[pl.ds(row, 32), pl.ds(col, 128)] = piece
+
+            return carry
+
+        lax.fori_loop(0, CHIPS, body, 0)
+
+    arrange(mc)
     for which, (buf, slow, quick, near, far) in enumerate(lines):
         drain(buf.at[pl.ds(0, 2)], s.fc_r.at[which])
-
-    def arrange(owner, carry):
-        x, y, c = owner // 8, (owner // 2) % 4, owner % 2
-        for p in range(2):
-            chunk = 2 * owner + p
-            row = pl.multiple_of((chunk // 7) * 32, 32)
-
-            @pl.when(chunk < 63)
-            def _():
-                for z in range(4):
-                    col = pl.multiple_of(z * UNITS + (chunk % 7) * 128, 128)
-                    piece = s.f0[y, c, x, z] if p == 0 else s.f1[x, c, y, z]
-                    s.fresh[pl.ds(row, 32), pl.ds(col, 128)] = piece
-
+    arrange(1 - mc)
+
+    in_e.wait()
+    s.raw[...] = dot(s.fresh[...], s.embv[...], NT)
+    lane = iota((16, 128), 1)
+    spot = [lane.astype(F32) + 128.0 * k for k in range(VOCAB // 128)]
+
+    def score(part, carry):
+        rows = pl.ds(pl.multiple_of(part * 16, 16), 16)
+        total = jnp.zeros((16, 128), F32)
+        picks = [jnp.zeros((16, 128), F32)] * TOPC
+        named = [s.idb[c, rows, :] for c in range(TOPC)]
+        for k in range(VOCAB // 128):
+            logits = 30.0 * jnp.tanh(s.raw[rows, k * 128:k * 128 + 128] * (1.0 / 30.0))
+            total = total + jnp.exp(logits)
+            picks = [jnp.where(named[c] == spot[k], logits, picks[c]) for c in range(TOPC)]
+        found = jnp.where(lane == TOPC, jnp.sum(total, 1, keepdims=True), 0.0)
+        for c in range(TOPC):
+            found = found + jnp.where(lane == c, jnp.sum(picks[c], 1, keepdims=True), 0.0)
+        s.cols[rows, :] = found
         return carry
 
-    lax.fori_loop(0, NB, arrange, 0)
-
-    in_e.wait()
-    tall = iota((16, MROWS), 0)
-
-    def score(tile, acc):
-        rows = pl.multiple_of(tile * 256, 256)
-        raw = dot(s.embv[pl.ds(rows, 256), :], s.fresh[...], NT)
-        logits = 30.0 * jnp.tanh(raw * (1.0 / 30.0))
-        acc = acc + jnp.where(tall == 0, jnp.sum(jnp.exp(logits), 0, keepdims=True), 0.0)
-        here = (iota((256, MROWS), 0) + tile * 256).astype(F32) + base
-        for c in range(TOPC):
-            chosen = jnp.where(here == ids[c:c + 1, :MROWS], logits, 0.0)
-            acc = acc + jnp.where(tall == c + 1, jnp.sum(chosen, 0, keepdims=True), 0.0)
-        return acc
-
-    stats = lax.fori_loop(0, 4, score, jnp.zeros((16, MROWS), F32))
-    s.sbuf[mz] = jnp.concatenate([stats, jnp.zeros((16, 384 - MROWS), F32)], 1)
+    s.cols[MROWS:, :] = jnp.zeros((384 - MROWS, 128), F32)
+    lax.fori_loop(0, MROWS // 16, score, 0)
+    stats = s.cols[...].T[:16]
+    tall = iota((16, 384), 0)
+
+    def pack(stats):
+        total = stats[TOPC:TOPC + 1]
+        high = total.astype(BF16).astype(F32)
+        middle = (total - high).astype(BF16).astype(F32)
+        low = total - high - middle
+        stats = jnp.where(tall == TOPC, high, stats)
+        stats = jnp.where(tall == TOPC + 1, middle, stats)
+        return jnp.where(tall == TOPC + 2, low, stats).astype(BF16)
+
+    def unpack(parts):
+        stats = parts[0].astype(F32)
+        for more in parts[1:]:
+            stats = stats + more.astype(F32)
+        total = stats[TOPC:TOPC + 1] + stats[TOPC + 1:TOPC + 2] + stats[TOPC + 2:TOPC + 3]
+        return jnp.where(tall == TOPC, total, stats)
+
+    def share(buf, spot, sems, targets):
+        own = buf.at[spot]
+        for where in targets:
+            remote(own, own, *sems, **where).start()
+
+    s.sbuf[mz * 2 + mc] = pack(stats)
+    targets = [{"blk": sibling}]
     for step in range(1, 4):
-        own = s.sbuf.at[mz]
-        remote(own, own, s.ss, s.sr, mp=z_of(step)).start()
+        targets += [{"mp": z_of(step)}, {"blk": sibling, "mp": z_of(step)}]
+    share(s.sbuf, mz * 2 + mc, (s.ss, s.sr), targets)
 
     for copy in in_g:
         copy.wait()
@@ -449,49 +517,24 @@
     for z in range(1, 4):
         attn = attn + s.zbuf[z].astype(F32)
     mean = jnp.sum(attn * attn, -1, keepdims=True) * (1.0 / D)
-    normed = attn * lax.rsqrt(mean + 1e-06) * s.gainv[...][None]
+    normed = attn * lax.rsqrt(mean + 1e-06) * s.gainv[...].reshape(1, 1, D)
     for t in range(3):
         s.nrm[6 * t:6 * t + 6, :] = normed[t, :6]
     out_ref[...] = (s.nrm[0:18, :] + s.residv[...].astype(F32)).astype(BF16)
 
-    drain(s.sbuf.at[pl.ds(0, 3)], s.sr)
-    summed = s.sbuf[0] + s.sbuf[1] + s.sbuf[2] + s.sbuf[3]
-    for t in range(3):
-        s.sown[t] = summed[:, t * 128:t * 128 + 128]
-    for t in range(3):
-        @pl.when(me != OWNERS[t])
-        def _():
-            remote(
-                s.sown.at[t], s.grecv.at[me], s.gs.at[t], s.gr, blk=OWNERS[t]
-            ).start()
-
-    for t in range(3):
-        @pl.when(me == OWNERS[t])
-        def _():
-            s.grecv[OWNERS[t]] = s.sown[t]
-            drain(s.grecv.at[pl.ds(0, NB - 1)], s.gr)
-            full = lax.fori_loop(
-                1, NB, lambda i, acc: acc + s.grecv[i], s.grecv[0]
-            )
-            s.rbuf[t] = full - jnp.log(full[0:1])
-
-            def tell(step, carry):
-                remote(
-                    s.rbuf.at[t], s.rbuf.at[t], s.rs, s.rr.at[t], blk=peer_of(step)
-                ).start()
-                return carry
-
-            lax.fori_loop(1, NB, tell, 0)
-            drain(s.grecv.at[pl.ds(0, NB - 1)], s.rs)
-
-    for t in range(3):
-        @pl.when(me != OWNERS[t])
-        def _():
-            drain(s.rbuf.at[t], s.rr.at[t])
-            drain(s.sown.at[t], s.gs.at[t])
-
-    stat_ref[...] = s.rbuf[...]
-
+    drain(s.sbuf.at[pl.ds(0, 7)], s.sr)
+    s.gbuf[chip] = pack(unpack([s.sbuf[i] for i in range(8)]))
+    share(
+        s.gbuf, chip, (s.gs, s.gr),
+        [{"blk": 2 * chip_of(step) + mc} for step in range(1, CHIPS)],
+    )
+    drain(s.gbuf.at[pl.ds(0, CHIPS - 1)], s.gr)
+    full = unpack([s.gbuf[i] for i in range(CHIPS)])
+    found = full - jnp.log(full[TOPC:TOPC + 1])
+    stat_ref[:, 0, :] = found[:TOPC, :ROWS]
+    stat_ref[:, 1, :] = pltpu.roll(found, 384 - ROWS, 1)[:TOPC, :ROWS]
+
+    drain(s.psib, s.pc_s)
     drain(s.precv, s.ps)
     drain(s.arecv.at[pl.ds(1, NB - 1)], s.as_)
     for which, (buf, slow, quick, near, far) in enumerate(lines):
@@ -511,7 +554,8 @@
 
     lax.fori_loop(0, GROUPS, sent_heads, 0)
     drain(s.zbuf.at[pl.ds(0, 3)], s.zs)
-    drain(s.sbuf.at[pl.ds(0, 3)], s.ss)
+    drain(s.sbuf.at[pl.ds(0, 7)], s.ss)
+    drain(s.gbuf.at[pl.ds(0, CHIPS - 1)], s.gs)
 
 
 def per_device(
@@ -525,7 +569,7 @@
         kernel,
         out_shape=(
             jax.ShapeDtypeStruct((18, D), BF16),
-            jax.ShapeDtypeStruct((3, 16, 128), F32),
+            jax.ShapeDtypeStruct((TOPC, 2, ROWS), F32),
         ),
         in_specs=[anywhere] * 7 + [scalar] * 3 + [anywhere] * 4,
         out_specs=(whole, whole),
@@ -534,12 +578,11 @@
             collective_id=0, has_side_effects=True, vmem_limit_bytes=60 << 20
         ),
     )(
-        hidden, medusa_w, embedding, cand_ids, tree_q, tree_key_value, prompt_key_value,
-        block_group, block_len, block_empty, parents, out_weight,
-        post_gain.reshape(1, D), resid,
+        hidden, medusa_w, embedding, cand_ids.transpose(2, 0, 1), tree_q, tree_key_value,
+        prompt_key_value, block_group, block_len, block_empty, parents, out_weight,
+        post_gain, resid,
     )
-    picked = jnp.concatenate([stats[t, 1:1 + TOPC] for t in range(3)], 1)[:, :MROWS]
-    return (picked.T.reshape(2, ROWS, TOPC), layer_out)
+    return (stats.transpose(1, 2, 0), layer_out)
 
 
 def solution(mesh):

time: 70 us -> 54.9 us (0.78)
  Pallas kernels: 61.2 us -> 49.2 us
  local copies, waits for them, and re-layouts: 5.86 us -> 2.93 us
    pallas_call x1, Pallas kernels: 61.2 us -> 49.2 us  [per_device(): pl.pallas_call(kernel, out_shape=(jax.ShapeDtypeStruct((18, D), BF16), ja...]
    reshape x2 -> x0, local copies, waits for them, and re-layouts: 2.02 us -> none  [the longest x1 1.33 us: per_device(): post_gain.reshape(1, D)]
    squeeze x1 -> x0, local copies, waits for them, and re-layouts: 0.74 us -> none  [per_device(): stats[t, 1:1 + TOPC]]
where the time goes in v2:
time: 54.9 us; the launch traced here: 54.7 us
  Pallas kernels  49.2 us (90%)
  local copies, waits for them, and re-layouts  2.93 us (5%)
  between operations  2.58 us (5%)
    pallas_call x1, Pallas kernels, per_device(): pl.pallas_call(kernel, out_shape=(jax.ShapeDtypeStruct((18, D), BF16), ja...  49.2 us
    unnamed x2, local copies, waits for them, and re-layouts  2.93 us

profile of v2, /device:TPU:1, one launch (start us, length us, event | category | flops | bytes accessed | tf_op | source)
XLA Modules:
  0.0 54.7 jit_solution(17623918658877711101)
XLA Ops:
  2.6 49.2 %shard_map.149 = (bf16[18,3584]{1,0:T(8,128)(2,1)}, f32[10,2,144]{2,1,0:T(2,128)}) custom-call(bf16[144,3584]{1,0:T(8,128)(2,1)} %hidden.1, bf16[2,112,896]{2,1,0:T(8,128)(2,1)} %medusa_w.1, bf16[1024,3584]{1,0:T(8,128)(2,1)} %embedding.1, s32[10,2,144]{2,1,0:T(2,128)} %bitcast.2, bf16[12,48,1024]{2,1,0:T(8,128)(2,1)} %tree_q.1, ...), custom_call_target="tpu_custom_call" | custom-call | tf_op jit(solution)/shard_map/pallas_call | solution.py:568
  51.8 1.3 %copy.21 = f32[2,144,10]{1,0,2:T(2,128)} copy(f32[2,144,10]{1,0,2:T(2,128)} %bitcast.3) | data formatting | bytes 23040
  53.1 1.6 %copy.22 = bf16[18,3584]{1,0:T(8,128)(2,1)} copy(bf16[18,3584]{1,0:T(8,128)(2,1)} %get-tuple-element.9) | data formatting | bytes 258048

commit v3 on v2

--- a/solution.py
+++ b/solution.py
@@ -72,7 +72,7 @@
     ("fa_s", pltpu.SemaphoreType.DMA((2,))),
     ("fa_r", pltpu.SemaphoreType.DMA((2, 3))),
     ("fb_s", pltpu.SemaphoreType.DMA((2,))),
-    ("fb_r", pltpu.SemaphoreType.DMA((2, 3))),
+    ("fb_r", pltpu.SemaphoreType.DMA((2, 3, 4))),
     ("fc_s", pltpu.SemaphoreType.DMA((2,))),
     ("fc_r", pltpu.SemaphoreType.DMA((2,))),
     ("fresh", pltpu.VMEM((MROWS, D), BF16)),
@@ -90,9 +90,11 @@
     ("zs", pltpu.SemaphoreType.DMA),
     ("zr", pltpu.SemaphoreType.DMA),
     ("nrm", pltpu.VMEM((24, D), F32)),
+    ("layer", pltpu.VMEM((18, D), BF16)),
+    ("sem_out", pltpu.SemaphoreType.DMA),
     ("idv", pltpu.VMEM((2, 16, 384), F32)),
     ("idb", pltpu.VMEM((TOPC, MROWS, 128), F32)),
-    ("raw", pltpu.VMEM((MROWS, VOCAB), F32)),
+    ("tally", pltpu.VMEM((TOPC + 1, MROWS, 128), F32)),
     ("cols", pltpu.VMEM((384, 128), F32)),
     ("sbuf", pltpu.VMEM((8, 16, 384), BF16)),
     ("ss", pltpu.SemaphoreType.DMA),
@@ -130,6 +132,12 @@
 
     def z_of(step):
         return lax.rem(mz + step, 4)
+
+    def x_peer(step):
+        return lax.rem(mx + step, 4) * 8 + my * 2 + mc
+
+    def y_peer(step):
+        return mx * 8 + lax.rem(my + step, 4) * 2 + mc
 
     def remote(src, dst, ss, rs, **where):
         return pltpu.make_async_remote_copy(
@@ -205,6 +213,14 @@
             barrier, inc=1, device_id={"blk": sibling, "mp": z_of(step)}, device_id_type=MESH
         )
 
+    for up in range(1, 4):
+        for step in range(1, 4):
+            for peer in (x_peer(step), y_peer(step)):
+                pl.semaphore_signal(
+                    barrier, inc=1, device_id={"blk": peer, "mp": z_of(up)},
+                    device_id_type=MESH,
+                )
+
     for copy in in_w:
         copy.wait()
     hwin = s.hwin[...]
@@ -219,7 +235,7 @@
                     product[u * 16:u * 16 + 16, lane * 128:lane * 128 + 128]
                 )
     s.pbuf[CHIPS - 1, 1, 1] = jnp.zeros((32, 128), BF16)
-    pl.semaphore_wait(barrier, NB - 1 + 6)
+    pl.semaphore_wait(barrier, NB - 1 + 6 + 18)
     remote(s.pbuf.at[:, 1 - mc], s.psib, s.pc_s, s.pc_r, blk=sibling).start()
     drain(s.psib, s.pc_r)
     s.psum[...] = (s.pbuf[:, mc].astype(F32) + s.psib[...].astype(F32)).astype(BF16)
@@ -281,21 +297,6 @@
     lax.fori_loop(1, NB, send_attention, 0)
     s.arecv[0] = s.abuf[me]
 
-    for copy in in_h:
-        copy.wait()
-    drain(s.precv, s.pr)
-    inner = lax.fori_loop(
-        0, CHIPS - 1,
-        lambda i, acc: acc + s.precv[i].astype(F32),
-        s.psum[chip].astype(F32),
-    )
-    fresh = (s.hown[...].astype(F32) + inner / (1.0 + jnp.exp(-inner))).astype(BF16)
-    s.f0[my, mc, mx, mz] = fresh[0]
-    s.f1[mx, mc, my, mz] = fresh[1]
-    for step in range(1, 4):
-        for which, own in enumerate((s.f0.at[my, mc, mx, mz], s.f1.at[mx, mc, my, mz])):
-            remote(own, own, s.fz_s.at[which], s.fz_r.at[which], mp=z_of(step)).start()
-
     for copy in in_t:
         copy.wait()
     for buf in (s.tqb, s.tkb, s.tvb):
@@ -329,29 +330,61 @@
         s.treen[4 * b:4 * b + 4] = numer.reshape(4, 8, HEAD)
         s.treed[4 * b:4 * b + 4] = denom.reshape(4, 8, 128)
 
-    def x_peer(step):
-        return lax.rem(mx + step, 4) * 8 + my * 2 + mc
-
-    def y_peer(step):
-        return mx * 8 + lax.rem(my + step, 4) * 2 + mc
-
+    for copy in in_h:
+        copy.wait()
+    drain(s.precv, s.pr)
+    inner = lax.fori_loop(
+        0, CHIPS - 1,
+        lambda i, acc: acc + s.precv[i].astype(F32),
+        s.psum[chip].astype(F32),
+    )
+    fresh = (s.hown[...].astype(F32) + inner / (1.0 + jnp.exp(-inner))).astype(BF16)
+    s.f0[my, mc, mx, mz] = fresh[0]
+    s.f1[mx, mc, my, mz] = fresh[1]
     lines = ((s.f0, my, mx, x_peer, y_peer), (s.f1, mx, my, y_peer, x_peer))
-    def pass_on(which, block, far):
+    for which, (buf, slow, quick, near, far) in enumerate(lines):
+        own = buf.at[slow, mc, quick, mz]
         for step in range(1, 4):
-            remote(
-                block, block, s.fb_s.at[which], s.fb_r.at[which, step - 1], blk=far(step)
-            ).start()
+            remote(own, own, s.fz_s.at[which], s.fz_r.at[which], mp=z_of(step)).start()
+    for step in range(1, 4):
+        for which, (buf, slow, quick, near, far) in enumerate(lines):
+            own = buf.at[slow, mc, quick, mz]
+            for up in range(4):
+                remote(
+                    own, own, s.fa_s.at[which], s.fa_r.at[which, step - 1],
+                    blk=near(step), mp=z_of(up),
+                ).start()
+
+    def to_sibling(which, block):
         remote(block, block, s.fc_s.at[which], s.fc_r.at[which], blk=sibling).start()
 
-    for which, (buf, slow, quick, near, far) in enumerate(lines):
-        drain(buf.at[slow, mc, quick, pl.ds(0, 3)], s.fz_r.at[which])
-        own = buf.at[slow, mc, quick]
+    def pass_on(part):
+        blocks = [
+            buf.at[slow, mc, lax.rem(quick - part + 4, 4)]
+            for buf, slow, quick, near, far in lines
+        ]
+        for step in (1, 3, 2):
+            for which, block in enumerate(blocks):
+                remote(
+                    block, block, s.fb_s.at[which], s.fb_r.at[which, step - 1, part],
+                    blk=lines[which][4](step),
+                ).start()
+        for which, block in enumerate(blocks):
+            to_sibling(which, block)
+
+    def far_came(part):
         for step in range(1, 4):
-            remote(
-                own, own, s.fa_s.at[which], s.fa_r.at[which, step - 1], blk=near(step)
-            ).start()
-    for which, (buf, slow, quick, near, far) in enumerate(lines):
-        pass_on(which, buf.at[slow, mc, quick], far)
+            for which, (buf, slow, quick, near, far) in enumerate(lines):
+                block = buf.at[
+                    lax.rem(slow - step + 4, 4), mc, lax.rem(quick - part + 4, 4)
+                ]
+                drain(block, s.fb_r.at[which, step - 1, part])
+                to_sibling(which, block)
+
+    def line_came():
+        for which, (buf, slow, quick, near, far) in enumerate(lines):
+            drain(buf.at[slow, mc, quick, pl.ds(0, 3)], s.fz_r.at[which])
+        pass_on(0)
 
     drain(s.arecv.at[pl.ds(1, NB - 1)], s.ar)
     for half in range(2):
@@ -396,11 +429,13 @@
 
     lax.fori_loop(0, GROUPS, send_heads, 0)
 
+    line_came()
     for step in range(1, 4):
         for which, (buf, slow, quick, near, far) in enumerate(lines):
             came = buf.at[slow, mc, lax.rem(quick - step + 4, 4)]
             drain(came, s.fa_r.at[which, step - 1])
-            pass_on(which, came, far)
+        pass_on(step)
+    far_came(0)
 
     in_o.wait()
     drain(s.hrecv, s.hr)
@@ -429,11 +464,8 @@
     for c in range(TOPC):
         s.idb[c] = jnp.broadcast_to(ids[:MROWS, c:c + 1], (MROWS, 128))
 
-    for step in range(1, 4):
-        for which, (buf, slow, quick, near, far) in enumerate(lines):
-            came = buf.at[lax.rem(slow - step + 4, 4), mc]
-            drain(came, s.fb_r.at[which, step - 1])
-            remote(came, came, s.fc_s.at[which], s.fc_r.at[which], blk=sibling).start()
+    for late in range(1, 4):
+        far_came(late)
 
     def arrange(core):
         def body(one, carry):
@@ -459,27 +491,46 @@
     arrange(1 - mc)
 
     in_e.wait()
-    s.raw[...] = dot(s.fresh[...], s.embv[...], NT)
     lane = iota((16, 128), 1)
     spot = [lane.astype(F32) + 128.0 * k for k in range(VOCAB // 128)]
 
-    def score(part, carry):
-        rows = pl.ds(pl.multiple_of(part * 16, 16), 16)
-        total = jnp.zeros((16, 128), F32)
-        picks = [jnp.zeros((16, 128), F32)] * TOPC
-        named = [s.idb[c, rows, :] for c in range(TOPC)]
-        for k in range(VOCAB // 128):
-            logits = 30.0 * jnp.tanh(s.raw[rows, k * 128:k * 128 + 128] * (1.0 / 30.0))
-            total = total + jnp.exp(logits)
-            picks = [jnp.where(named[c] == spot[k], logits, picks[c]) for c in range(TOPC)]
-        found = jnp.where(lane == TOPC, jnp.sum(total, 1, keepdims=True), 0.0)
-        for c in range(TOPC):
-            found = found + jnp.where(lane == c, jnp.sum(picks[c], 1, keepdims=True), 0.0)
-        s.cols[rows, :] = found
-        return carry
+    def raw_tile(tile):
+        return dot(s.fresh[...], s.embv[tile * 256:tile * 256 + 256, :], NT)
+
+    def score(raw, tile):
+        for strip in range(MROWS // 16):
+            rows = slice(strip * 16, strip * 16 + 16)
+            if tile == 0:
+                total = jnp.zeros((16, 128), F32)
+                picks = [total] * TOPC
+            else:
+                total = s.tally[TOPC, rows, :]
+                picks = [s.tally[c, rows, :] for c in range(TOPC)]
+            for k in range(2):
+                logits = 30.0 * jnp.tanh(raw[rows, k * 128:k * 128 + 128] * (1.0 / 30.0))
+                total = total + jnp.exp(logits)
+                picks = [
+                    jnp.where(s.idb[c, rows, :] == spot[2 * tile + k], logits, picks[c])
+                    for c in range(TOPC)
+                ]
+            if tile < 3:
+                s.tally[TOPC, rows, :] = total
+                for c in range(TOPC):
+                    s.tally[c, rows, :] = picks[c]
+            else:
+                found = jnp.where(lane == TOPC, jnp.sum(total, 1, keepdims=True), 0.0)
+                for c in range(TOPC):
+                    row_sum = jnp.sum(picks[c], 1, keepdims=True)
+                    found = found + jnp.where(lane == c, row_sum, 0.0)
+                s.cols[rows, :] = found
 
     s.cols[MROWS:, :] = jnp.zeros((384 - MROWS, 128), F32)
-    lax.fori_loop(0, MROWS // 16, score, 0)
+    raw = raw_tile(0)
+    for tile in range(1, 4):
+        ahead = raw_tile(tile)
+        score(raw, tile - 1)
+        raw = ahead
+    score(raw, 3)
     stats = s.cols[...].T[:16]
     tall = iota((16, 384), 0)
 
@@ -520,7 +571,9 @@
     normed = attn * lax.rsqrt(mean + 1e-06) * s.gainv[...].reshape(1, 1, D)
     for t in range(3):
         s.nrm[6 * t:6 * t + 6, :] = normed[t, :6]
-    out_ref[...] = (s.nrm[0:18, :] + s.residv[...].astype(F32)).astype(BF16)
+    s.layer[...] = (s.nrm[0:18, :] + s.residv[...].astype(F32)).astype(BF16)
+    leave = pltpu.make_async_copy(s.layer, out_ref, s.sem_out)
+    leave.start()
 
     drain(s.sbuf.at[pl.ds(0, 7)], s.sr)
     s.gbuf[chip] = pack(unpack([s.sbuf[i] for i in range(8)]))
@@ -533,6 +586,8 @@
     found = full - jnp.log(full[TOPC:TOPC + 1])
     stat_ref[:, 0, :] = found[:TOPC, :ROWS]
     stat_ref[:, 1, :] = pltpu.roll(found, 384 - ROWS, 1)[:TOPC, :ROWS]
+
+    leave.wait()
 
     drain(s.psib, s.pc_s)
     drain(s.precv, s.ps)
@@ -572,7 +627,7 @@
             jax.ShapeDtypeStruct((TOPC, 2, ROWS), F32),
         ),
         in_specs=[anywhere] * 7 + [scalar] * 3 + [anywhere] * 4,
-        out_specs=(whole, whole),
+        out_specs=(anywhere, whole),
         scratch_shapes=[kind for _, kind in SCRATCH],
         compiler_params=pltpu.CompilerParams(
             collective_id=0, has_side_effects=True, vmem_limit_bytes=60 << 20

time: 54.9 us -> 53.5 us (0.974)
  Pallas kernels: 49.2 us -> 47.6 us
    pallas_call x1, Pallas kernels: 49.2 us -> 47.6 us  [per_device(): pl.pallas_call(kernel, out_shape=(jax.ShapeDtypeStruct((18, D), BF16), ja...]
where the time goes in v3:
time: 53.5 us; the launch traced here: 53.1 us
  Pallas kernels  47.6 us (89%)
  local copies, waits for them, and re-layouts  2.93 us (5%)
  between operations  2.58 us (5%)
    pallas_call x1, Pallas kernels, per_device(): pl.pallas_call(kernel, out_shape=(jax.ShapeDtypeStruct((18, D), BF16), ja...  47.6 us
    unnamed x2, local copies, waits for them, and re-layouts  2.93 us

profile of v3, /device:TPU:1, one launch (start us, length us, event | category | flops | bytes accessed | tf_op | source)
XLA Modules:
  0.0 53.1 jit_solution(14967018822861443696)
XLA Ops:
  2.6 47.6 %shard_map.149 = (bf16[18,3584]{1,0:T(8,128)(2,1)}, f32[10,2,144]{2,1,0:T(2,128)}) custom-call(bf16[144,3584]{1,0:T(8,128)(2,1)} %hidden.1, bf16[2,112,896]{2,1,0:T(8,128)(2,1)} %medusa_w.1, bf16[1024,3584]{1,0:T(8,128)(2,1)} %embedding.1, s32[10,2,144]{2,1,0:T(2,128)} %bitcast.2, bf16[12,48,1024]{2,1,0:T(8,128)(2,1)} %tree_q.1, ...), custom_call_target="tpu_custom_call" | custom-call | tf_op jit(solution)/shard_map/pallas_call | solution.py:623
  50.2 1.3 %copy.21 = f32[2,144,10]{1,0,2:T(2,128)} copy(f32[2,144,10]{1,0,2:T(2,128)} %bitcast.3) | data formatting | bytes 23040
  51.5 1.6 %copy.22 = bf16[18,3584]{1,0:T(8,128)(2,1)} copy(bf16[18,3584]{1,0:T(8,128)(2,1)} %get-tuple-element.9) | data formatting | bytes 258048

commit v4 on v3

--- a/solution.py
+++ b/solution.py
@@ -57,14 +57,14 @@
     ("gainv", pltpu.VMEM((D,), F32)),
     ("residv", pltpu.VMEM((18, D), BF16)),
     ("sem_in", pltpu.SemaphoreType.DMA((20,))),
-    ("pbuf", pltpu.VMEM((CHIPS, 2, 2, 32, 128), BF16)),
-    ("psib", pltpu.VMEM((CHIPS, 2, 32, 128), BF16)),
-    ("psum", pltpu.VMEM((CHIPS, 2, 32, 128), BF16)),
-    ("precv", pltpu.VMEM((CHIPS - 1, 2, 32, 128), BF16)),
-    ("pc_s", pltpu.SemaphoreType.DMA),
-    ("pc_r", pltpu.SemaphoreType.DMA),
-    ("ps", pltpu.SemaphoreType.DMA),
-    ("pr", pltpu.SemaphoreType.DMA),
+    ("pbuf", pltpu.VMEM((2, CHIPS, 2, 32, 128), BF16)),
+    ("psib", pltpu.VMEM((2, CHIPS, 32, 128), BF16)),
+    ("psum", pltpu.VMEM((2, CHIPS, 32, 128), BF16)),
+    ("precv", pltpu.VMEM((2, CHIPS - 1, 32, 128), BF16)),
+    ("pc_s", pltpu.SemaphoreType.DMA((2,))),
+    ("pc_r", pltpu.SemaphoreType.DMA((2,))),
+    ("ps", pltpu.SemaphoreType.DMA((2,))),
+    ("pr", pltpu.SemaphoreType.DMA((2,))),
     ("f0", pltpu.VMEM((4, 2, 4, 4, 32, 128), BF16)),
     ("f1", pltpu.VMEM((4, 2, 4, 4, 32, 128), BF16)),
     ("fz_s", pltpu.SemaphoreType.DMA((2,))),
@@ -147,6 +147,31 @@
 
     def drain(ref, sem):
         pltpu.make_async_copy(ref, ref, sem).wait()
+
+    barrier = pltpu.get_barrier_semaphore()
+
+    def greet(step, carry):
+        pl.semaphore_signal(
+            barrier, inc=1, device_id={"blk": peer_of(step)}, device_id_type=MESH
+        )
+        return carry
+
+    lax.fori_loop(1, NB, greet, 0)
+    for step in range(1, 4):
+        pl.semaphore_signal(
+            barrier, inc=1, device_id={"mp": z_of(step)}, device_id_type=MESH
+        )
+        pl.semaphore_signal(
+            barrier, inc=1, device_id={"blk": sibling, "mp": z_of(step)}, device_id_type=MESH
+        )
+
+    for up in range(1, 4):
+        for step in range(1, 4):
+            for peer in (x_peer(step), y_peer(step)):
+                pl.semaphore_signal(
+                    barrier, inc=1, device_id={"blk": peer, "mp": z_of(up)},
+                    device_id_type=MESH,
+                )
 
     inputs = []
 
@@ -196,31 +221,6 @@
     in_g = [fetch(post_gain, s.gainv), fetch(resid, s.residv)]
     in_e = fetch(embedding, s.embv)
 
-    barrier = pltpu.get_barrier_semaphore()
-
-    def greet(step, carry):
-        pl.semaphore_signal(
-            barrier, inc=1, device_id={"blk": peer_of(step)}, device_id_type=MESH
-        )
-        return carry
-
-    lax.fori_loop(1, NB, greet, 0)
-    for step in range(1, 4):
-        pl.semaphore_signal(
-            barrier, inc=1, device_id={"mp": z_of(step)}, device_id_type=MESH
-        )
-        pl.semaphore_signal(
-            barrier, inc=1, device_id={"blk": sibling, "mp": z_of(step)}, device_id_type=MESH
-        )
-
-    for up in range(1, 4):
-        for step in range(1, 4):
-            for peer in (x_peer(step), y_peer(step)):
-                pl.semaphore_signal(
-                    barrier, inc=1, device_id={"blk": peer, "mp": z_of(up)},
-                    device_id_type=MESH,
-                )
-
     for copy in in_w:
         copy.wait()
     hwin = s.hwin[...]
@@ -231,21 +231,24 @@
             for lane in range(7):
                 chunk = (unit // 2) * 7 + lane
                 low = (unit % 2) * 16
-                s.pbuf[chunk // 4, chunk // 2 % 2, chunk % 2, low:low + 16, :] = (
+                s.pbuf[chunk % 2, chunk // 4, chunk // 2 % 2, low:low + 16, :] = (
                     product[u * 16:u * 16 + 16, lane * 128:lane * 128 + 128]
                 )
-    s.pbuf[CHIPS - 1, 1, 1] = jnp.zeros((32, 128), BF16)
+    s.pbuf[1, CHIPS - 1, 1] = jnp.zeros((32, 128), BF16)
     pl.semaphore_wait(barrier, NB - 1 + 6 + 18)
-    remote(s.pbuf.at[:, 1 - mc], s.psib, s.pc_s, s.pc_r, blk=sibling).start()
-    drain(s.psib, s.pc_r)
-    s.psum[...] = (s.pbuf[:, mc].astype(F32) + s.psib[...].astype(F32)).astype(BF16)
-
-    def send_product(step, carry):
-        to = chip_of(step)
-        remote(s.psum.at[to], s.precv.at[step - 1], s.ps, s.pr, blk=2 * to + mc).start()
-        return carry
-
-    lax.fori_loop(1, CHIPS, send_product, 0)
+    for p in range(2):
+        remote(
+            s.pbuf.at[p, :, 1 - mc], s.psib.at[p], s.pc_s.at[p], s.pc_r.at[p], blk=sibling
+        ).start()
+    for p in range(2):
+        drain(s.psib.at[p], s.pc_r.at[p])
+        s.psum[p] = (s.pbuf[p, :, mc].astype(F32) + s.psib[p].astype(F32)).astype(BF16)
+        for step in range(1, CHIPS):
+            to = chip_of(step)
+            remote(
+                s.psum.at[p, to], s.precv.at[p, step - 1], s.ps.at[p], s.pr.at[p],
+                blk=2 * to + mc,
+            ).start()
 
     group = block_group[0]
     limit = jnp.where(block_empty[0] == 0, block_len[0], 0)
@@ -332,23 +335,18 @@
 
     for copy in in_h:
         copy.wait()
-    drain(s.precv, s.pr)
-    inner = lax.fori_loop(
-        0, CHIPS - 1,
-        lambda i, acc: acc + s.precv[i].astype(F32),
-        s.psum[chip].astype(F32),
-    )
-    fresh = (s.hown[...].astype(F32) + inner / (1.0 + jnp.exp(-inner))).astype(BF16)
-    s.f0[my, mc, mx, mz] = fresh[0]
-    s.f1[mx, mc, my, mz] = fresh[1]
     lines = ((s.f0, my, mx, x_peer, y_peer), (s.f1, mx, my, y_peer, x_peer))
     for which, (buf, slow, quick, near, far) in enumerate(lines):
+        drain(s.precv.at[which], s.pr.at[which])
+        inner = s.psum[which, chip].astype(F32)
+        for i in range(CHIPS - 1):
+            inner = inner + s.precv[which, i].astype(F32)
+        fresh = s.hown[which].astype(F32) + inner / (1.0 + jnp.exp(-inner))
+        buf[slow, mc, quick, mz] = fresh.astype(BF16)
         own = buf.at[slow, mc, quick, mz]
         for step in range(1, 4):
             remote(own, own, s.fz_s.at[which], s.fz_r.at[which], mp=z_of(step)).start()
-    for step in range(1, 4):
-        for which, (buf, slow, quick, near, far) in enumerate(lines):
-            own = buf.at[slow, mc, quick, mz]
+        for step in range(1, 4):
             for up in range(4):
                 remote(
                     own, own, s.fa_s.at[which], s.fa_r.at[which, step - 1],
@@ -467,10 +465,10 @@
     for late in range(1, 4):
         far_came(late)
 
-    def arrange(core):
+    def arrange(core, lots):
         def body(one, carry):
             x, y = one // 4, one % 4
-            for p in range(2):
+            for p in lots:
                 chunk = 4 * one + 2 * core + p
                 row = pl.multiple_of((chunk // 7) * 32, 32)
 
@@ -485,10 +483,10 @@
 
         lax.fori_loop(0, CHIPS, body, 0)
 
-    arrange(mc)
+    arrange(mc, (0, 1))
     for which, (buf, slow, quick, near, far) in enumerate(lines):
         drain(buf.at[pl.ds(0, 2)], s.fc_r.at[which])
-    arrange(1 - mc)
+        arrange(1 - mc, (which,))
 
     in_e.wait()
     lane = iota((16, 128), 1)
@@ -589,8 +587,9 @@
 
     leave.wait()
 
-    drain(s.psib, s.pc_s)
-    drain(s.precv, s.ps)
+    for p in range(2):
+        drain(s.psib.at[p], s.pc_s.at[p])
+        drain(s.precv.at[p], s.ps.at[p])
     drain(s.arecv.at[pl.ds(1, NB - 1)], s.as_)
     for which, (buf, slow, quick, near, far) in enumerate(lines):
         drain(buf.at[slow, mc, quick, pl.ds(0, 3)], s.fz_s.at[which])
@@ -618,6 +617,14 @@
     block_group, block_len, block_empty, parents, out_weight, post_gain, resid,
 ):
     anywhere = pl.BlockSpec(memory_space=pl.ANY)
+    stay = lambda array: pltpu.with_memory_space_constraint(array, pltpu.HBM)
+    hidden, medusa_w, embedding, cand_ids, tree_q, tree_key_value, prompt_key_value = map(
+        stay, (hidden, medusa_w, embedding, cand_ids.transpose(2, 0, 1), tree_q,
+               tree_key_value, prompt_key_value)
+    )
+    parents, out_weight, post_gain, resid = map(
+        stay, (parents, out_weight, post_gain, resid)
+    )
     scalar = pl.BlockSpec(memory_space=pltpu.SMEM)
     whole = pl.BlockSpec(memory_space=pltpu.VMEM)
     layer_out, stats = pl.pallas_call(
@@ -630,10 +637,10 @@
         out_specs=(anywhere, whole),
         scratch_shapes=[kind for _, kind in SCRATCH],
         compiler_params=pltpu.CompilerParams(
-            collective_id=0, has_side_effects=True, vmem_limit_bytes=60 << 20
+            collective_id=0, has_side_effects=True, vmem_limit_bytes=44 << 20
         ),
     )(
-        hidden, medusa_w, embedding, cand_ids.transpose(2, 0, 1), tree_q, tree_key_value,
+        hidden, medusa_w, embedding, cand_ids, tree_q, tree_key_value,
         prompt_key_value, block_group, block_len, block_empty, parents, out_weight,
         post_gain, resid,
     )

time: 53.5 us -> 50.8 us (0.950)
  local copies, waits for them, and re-layouts: 2.93 us -> 1.28 us
  Pallas kernels: 47.6 us -> 46.6 us
    unnamed x2, local copies, waits for them, and re-layouts: 2.93 us -> 1.28 us
    pallas_call x1, Pallas kernels: 47.6 us -> 46.6 us  [per_device(): pl.pallas_call(kernel, out_shape=(jax.ShapeDtypeStruct((18, D), BF16), ja...]
where the time goes in v4:
time: 50.8 us; the launch traced here: 50.4 us
  Pallas kernels  46.6 us (92%)
  between operations  2.58 us (5%)
  local copies, waits for them, and re-layouts  1.28 us (3%)
    pallas_call x1, Pallas kernels, per_device(): pl.pallas_call(kernel, out_shape=(jax.ShapeDtypeStruct((18, D), BF16), ja...  46.6 us
    unnamed x2, local copies, waits for them, and re-layouts  1.28 us

profile of v4, /device:TPU:1, one launch (start us, length us, event | category | flops | bytes accessed | tf_op | source)
XLA Modules:
  0.0 50.4 jit_solution(5307536417767912309)
XLA Ops:
  2.6 46.6 %shard_map.149 = (bf16[18,3584]{1,0:T(8,128)(2,1)S(1)}, f32[10,2,144]{2,1,0:T(2,128)S(1)}) custom-call(bf16[144,3584]{1,0:T(8,128)(2,1)} %hidden.1, bf16[2,112,896]{2,1,0:T(8,128)(2,1)} %medusa_w.1, bf16[1024,3584]{1,0:T(8,128)(2,1)} %embedding.1, s32[10,2,144]{2,1,0:T(2,128)} %bitcast.3, bf16[12,48,1024]{2,1,0:T(8,128)(2,1)} %tree_q.1, ...), custom_call_target="tpu_custom_call" | custom-call | tf_op jit(solution)/shard_map/pallas_call | solution.py:630
  49.1 0.6 %copy.21 = f32[2,144,10]{1,0,2:T(2,128)} copy(f32[2,144,10]{1,0,2:T(2,128)S(1)} %bitcast.2) | data formatting | bytes 23040
  49.8 0.7 %copy.22 = bf16[18,3584]{1,0:T(8,128)(2,1)} copy(bf16[18,3584]{1,0:T(8,128)(2,1)S(1)} %get-tuple-element.9) | data formatting | bytes 258048
